TPU v7x, 128 devices: a whole 4x4x4 slice. The times are simulated.
128 devices in a mesh: seq: 16 (over y, x), tensor: 8 (over z, core).
Axes of the slice: x: 4, y: 4, z: 4, core: 2. Of those that a mesh axis runs over, the one named last changes fastest.
Arguments:
- tokens: bfloat16 [2048, 4096], P('seq'), may hold values from -8 to 8
- segment_ids: int32 [2048], replicated, may hold values from -1 to 14, as said below
- routes: int32 [2048, 2], P('seq'), may hold values from 0 to 7, all different within a row; in each aligned block of 128 rows (0 to 127, 128 to 255, ...) at most 64 rows name the same one
- owners: int32 [15], replicated, may hold values from 0 to 15
- gain_attn: float32 [4096], replicated, may hold values from 0.5 to 1.5
- w_query: bfloat16 [4096, 4096], P(None, 'tensor'), may hold values from -1 to 1
- w_kv: bfloat16 [4096, 2048], P(None, 'tensor'), may hold values from -1 to 1
- w_out: bfloat16 [4096, 4096], P('tensor'), may hold values from -0.09375 to 0.09375
- gain_moe: float32 [4096], replicated, may hold values from 0.5 to 1.5
- w_router: float32 [4096, 8], replicated, may hold values from -0.09375 to 0.09375
- w_gate: bfloat16 [4096, 65536], P(None, ('seq', 'tensor')), may hold values from -0.09375 to 0.09375
- w_up: bfloat16 [4096, 65536], P(None, ('seq', 'tensor')), may hold values from -0.09375 to 0.09375
- w_down: bfloat16 [65536, 4096], P(('seq', 'tensor')), may hold values from -0.0625 to 0.0625
Outputs:
- layer_out: bfloat16 [2048, 4096], P('seq', 'tensor')
- kv_cache: bfloat16 [32768, 2048], P('seq', 'tensor')
Inputs may be any that keep to these rules, and one draw needn't show every extreme that they name: `segment_ids`: tokens 0 to 1599 form segment 0; segments 1 to 14 follow in order, each of 8 to 31 tokens; all later tokens are -1. `routes`: in each aligned block of 128 rows no expert is named by more than 64 rows; the two experts of a row differ.
All inputs are finite; a program needn't handle non-finite values.
Results may differ from a plain program's by a relative error of at most 0.014.
Values may be sent and summed in bfloat16 or wider, within the bound.
No kernel may reach another device: no remote copies, remote signals or barrier semaphores. Data moves between devices by JAX's collectives and lax.ppermute only.
A program may use at most 128 MiB of HBM per device.

v0:
```python
import functools

import jax
import jax.numpy as jnp
from jax import lax
from jax.experimental import pallas as pl
from jax.experimental.pallas import tpu as pltpu
from jax.sharding import PartitionSpec as P


HEADS = 32
KV_HEADS = 8
HEAD_DIM = 128
EXPERTS = 8
EPS = 1e-05
THETA = 1000000.0
FLOOR = -1e30
NZ = 4
MIB = 1024 * 1024
F32 = jnp.float32
BF16 = jnp.bfloat16


VMEM_SPEC = pl.BlockSpec(memory_space=pltpu.VMEM)
ANY_SPEC = pl.BlockSpec(memory_space=pl.ANY)
HBM_SPEC = pl.BlockSpec(memory_space=pltpu.HBM)
SMEM_SPEC = pl.BlockSpec(memory_space=pltpu.SMEM)


def z_perm(step):
    return [(2 * z + c, 2 * ((z + step) % NZ) + c) for z in range(NZ) for c in range(2)]


def core_perm():
    return [(t, t ^ 1) for t in range(2 * NZ)]


def send_z(value, step):
    return lax.ppermute(value, "tensor", z_perm(step))


def send_core(value):
    return lax.ppermute(value, "tensor", core_perm())


def rotate(values, cosine, sine):
    half = values.shape[-1] // 2
    first = values[..., :half]
    second = values[..., half:]
    return jnp.concatenate(
        [first * cosine - second * sine, second * cosine + first * sine], axis=-1
    )


def attention_kernel(ids, first_ref, q_ref, start_ref, kv_ref, w_hbm, mine_ref, sib_ref, w_ref, sem):
    copy = pltpu.make_async_copy(w_hbm, w_ref, sem)
    copy.start()
    rows, dim = start_ref.shape[0], HEAD_DIM
    group = q_ref.shape[0] // rows
    count = kv_ref.shape[0]
    both = 2 * rows
    inner = lax.broadcasted_iota(jnp.int32, (both, count), 0)
    query = first_ref[0] + jnp.where(inner >= rows, inner - rows, inner)
    key = lax.broadcasted_iota(jnp.int32, (both, count), 1)
    start = jnp.concatenate([start_ref[...], start_ref[...]], axis=0)
    mask = (key <= query) & (key >= start)
    scale = HEAD_DIM ** (-0.5)
    heads = []
    for g in range(0, group, 2):
        q = q_ref[g * rows : (g + 2) * rows, :]
        s = lax.dot_general(
            q, kv_ref[:, :dim], (((1,), (1,)), ((), ())), preferred_element_type=F32
        )
        s = jnp.where(mask, s * scale, FLOOR)
        w = jnp.exp(s - jnp.max(s, axis=1, keepdims=True))
        mass = jnp.sum(w, axis=1, keepdims=True)
        acc = jnp.dot(w.astype(BF16), kv_ref[:, dim:], preferred_element_type=F32)
        acc = (acc / mass).astype(BF16)
        heads += [acc[:rows], acc[rows:]]
    attended = jnp.concatenate(heads, axis=1)
    copy.wait()
    share = mine_ref.shape[2]

    def project(at):
        w = w_ref[:, pl.ds(pl.multiple_of(at * share, share), share)]
        return jnp.dot(attended, w, preferred_element_type=F32)

    def body(d, carry):
        sib_ref[d] = project(ids[4 + d]).astype(BF16)
        mine_ref[d] = project(ids[d])
        return carry

    lax.fori_loop(0, NZ, body, 0)


def attend(ids, first, q, start, kv, w_out, share):
    rows = start.shape[0]
    return pl.pallas_call(
        attention_kernel,
        out_shape=(
            jax.ShapeDtypeStruct((NZ, rows, share), F32),
            jax.ShapeDtypeStruct((NZ, rows, share), BF16),
        ),
        in_specs=[SMEM_SPEC, SMEM_SPEC, VMEM_SPEC, VMEM_SPEC, VMEM_SPEC, HBM_SPEC],
        out_specs=(VMEM_SPEC, VMEM_SPEC),
        scratch_shapes=[pltpu.VMEM(w_out.shape, BF16), pltpu.SemaphoreType.DMA],
        compiler_params=pltpu.CompilerParams(vmem_limit_bytes=24 * MIB),
    )(ids, first, q, start, kv, w_out)


def ffn_kernel(count, pieces_to_outs, ids, gain_ref, *refs):
    pieces, refs = refs[:count], refs[count:]
    copies = []
    if len(refs) > 9:
        sources, outs, held, (xs_ref, act_ref, sems) = refs[:6], refs[6:10], refs[10:13], refs[13:]
        gate_ref, up_ref, down_ref = held
        places = [gate_ref.at[0], up_ref.at[0], gate_ref.at[1], up_ref.at[1]]
        places += [down_ref.at[0], down_ref.at[1]]
        copies = [
            pltpu.make_async_copy(source, ref, sems.at[i])
            for i, (source, ref) in enumerate(zip(sources, places, strict=True))
        ]
    else:
        gate_ref, up_ref, down_ref = refs[:3]
        outs, (xs_ref, act_ref) = refs[3:7], refs[7:]
    for copy in copies[:3]:
        copy.start()

    def arrived(i):
        if copies:
            copies[i].wait()
            if i + 3 < len(copies):
                copies[i + 3].start()

    rows, share = pieces[0].shape
    half = rows // 2
    width = gate_ref.shape[1]
    tile = 32

    for side in range(2):
        chosen = [(pieces[k], 0, k) for k in range(3)]
        chosen += [(pieces[3 + side], side * half, 3) if len(pieces) > 4 else (pieces[3], 0, 3)]

        def norm(i, carry):
            at_row = pl.multiple_of(side * half + i * tile, tile)
            total = jnp.zeros((tile, share), F32)
            for ref, low, _ in chosen:
                v = ref[pl.ds(pl.multiple_of(at_row - low, tile), tile), :].astype(F32)
                total = total + v * v
            mean = jnp.sum(total, axis=1, keepdims=True) * (1.0 / width)
            scale = lax.rsqrt(mean + EPS)
            for ref, low, k in chosen:
                at = ids[k]
                v = ref[pl.ds(pl.multiple_of(at_row - low, tile), tile), :].astype(F32)
                v = v * scale * gain_ref[pl.ds(at, 1), :]
                column = pl.ds(pl.multiple_of(at * share, share), share)
                xs_ref[pl.ds(at_row, tile), column] = v.astype(BF16)
            return carry

        lax.fori_loop(0, half // tile, norm, 0)

    for k in range(2):
        arrived(2 * k)
        gate = jnp.dot(xs_ref[...], gate_ref[k], preferred_element_type=F32)
        arrived(2 * k + 1)
        up = jnp.dot(xs_ref[...], up_ref[k], preferred_element_type=F32)
        act_ref[k] = (gate / (1.0 + jnp.exp(-gate)) * up).astype(BF16)
    arrived(4)
    arrived(5)
    for d in (2, 1, 3, 0):
        column = pl.ds(pl.multiple_of(ids[4 + d] * share, share), share)
        total = jnp.dot(act_ref[0], down_ref[0, :, column], preferred_element_type=F32)
        total = total + jnp.dot(act_ref[1], down_ref[1, :, column], preferred_element_type=F32)
        total = total.astype(BF16)
        for part in range(2):
            at_row = slice(part * half, (part + 1) * half)
            outs[pieces_to_outs[d][part]][at_row, :] = total[at_row, :]


def ffn(ids, gain, weights, pieces, targets):
    rows, share = pieces[0].shape
    depth, width = weights[0].shape[-2:]
    outs = (jax.ShapeDtypeStruct((rows, share), BF16),) * 4
    scratch = [pltpu.VMEM((rows, depth), BF16), pltpu.VMEM((2, rows, width), BF16)]
    spec = VMEM_SPEC
    if len(weights) == 6:
        shapes = (weights[0].shape, weights[1].shape, weights[4].shape)
        outs += tuple(jax.ShapeDtypeStruct((2,) + shape, BF16) for shape in shapes)
        scratch.append(pltpu.SemaphoreType.DMA((6,)))
        spec = HBM_SPEC
    return pl.pallas_call(
        functools.partial(ffn_kernel, len(pieces), targets),
        out_shape=outs,
        in_specs=[SMEM_SPEC] + [VMEM_SPEC] * (1 + len(pieces)) + [spec] * len(weights),
        out_specs=(VMEM_SPEC,) * len(outs),
        scratch_shapes=scratch,
        compiler_params=pltpu.CompilerParams(vmem_limit_bytes=16 * MIB),
    )(ids, gain, *pieces, *weights)


def in_vmem(value):
    return pltpu.with_memory_space_constraint(value, pltpu.VMEM)


def in_hbm(value):
    return pltpu.with_memory_space_constraint(value, pltpu.HBM)


def gather_direct(own):
    below = in_vmem(send_z(own, 1))
    above = in_vmem(send_z(own, -1))
    far = in_vmem(send_z(own, 2))
    return [own, below, above, far]


def split_kernel(below_ref, above_ref, low_ref, high_ref):
    half = low_ref.shape[0]
    low_ref[...] = below_ref[:half, :]
    high_ref[...] = above_ref[half:, :]


def gather_ring(own):
    half = own.shape[0] // 2
    below = in_vmem(send_z(own, 1))
    above = in_vmem(send_z(own, -1))
    low, high = local_call(split_kernel, (below, above), (half, half))
    far_a = in_vmem(send_z(low, 1))
    far_b = in_vmem(send_z(high, -1))
    return [own, below, above, far_a, far_b]


def relay_kernel(relay_ref, below_ref, above_ref, low_ref, high_ref):
    half = low_ref.shape[0]
    low = relay_ref[:half, :].astype(F32) + below_ref[:half, :].astype(F32)
    high = relay_ref[half:, :].astype(F32) + above_ref[half:, :].astype(F32)
    low_ref[...] = low.astype(BF16)
    high_ref[...] = high.astype(BF16)


def end_kernel(rest_ref, below_ref, above_ref, low_ref, high_ref, out_ref):
    half = low_ref.shape[0]
    total = rest_ref[...].astype(F32)
    first = total[:half] + above_ref[:half, :].astype(F32) + low_ref[...].astype(F32)
    second = total[half:] + below_ref[half:, :].astype(F32) + high_ref[...].astype(F32)
    out_ref[:half, :] = first.astype(BF16)
    out_ref[half:, :] = second.astype(BF16)


def local_call(kernel, args, heights):
    share = args[0].shape[1]
    return pl.pallas_call(
        kernel,
        out_shape=tuple(jax.ShapeDtypeStruct((height, share), BF16) for height in heights),
        in_specs=[VMEM_SPEC] * len(args),
        out_specs=(VMEM_SPEC,) * len(heights),
        compiler_params=pltpu.CompilerParams(vmem_limit_bytes=16 * MIB),
    )(*args)


def sum_kernel(*refs):
    total = refs[0][...].astype(F32)
    for ref in refs[1:-1]:
        total = total + ref[...].astype(F32)
    refs[-1][...] = total.astype(BF16)


def scatter_direct(near, above, far, rest):
    moved = [in_vmem(send_z(v, d)) for v, d in ((near, 1), (above, -1), (far, 2))]
    return local_call(sum_kernel, (in_hbm(rest), *moved), (rest.shape[0],))[0]


def scatter_ring(up, down, relay, rest):
    rows = up.shape[0]
    half = rows // 2
    from_below = in_vmem(send_z(up, 1))
    from_above = in_vmem(send_z(down, -1))
    low, high = local_call(
        relay_kernel, (in_hbm(relay), from_below, from_above), (half, half)
    )
    low = in_hbm(send_z(in_hbm(low), 1))
    high = in_hbm(send_z(in_hbm(high), -1))
    moved = (from_below, from_above, low, high)
    return local_call(end_kernel, (in_hbm(rest), *moved), (rows,))[0]


def cache_kernel(slot_ref, kv_ref, out_ref):
    rows, total = out_ref.shape[0], kv_ref.shape[0]
    place = pl.program_id(0) * rows + lax.broadcasted_iota(jnp.int32, (rows, total), 0)
    take = jnp.where(place == slot_ref[...], 1.0, 0.0).astype(BF16)
    out_ref[...] = jnp.dot(take, kv_ref[...], preferred_element_type=F32).astype(BF16)


def fill_cache(slot, kv):
    total, width = kv.shape
    rows = 256
    return pl.pallas_call(
        cache_kernel,
        grid=(total // rows,),
        out_shape=jax.ShapeDtypeStruct((total, width), BF16),
        in_specs=[
            pl.BlockSpec((1, total), lambda i: (0, 0)),
            pl.BlockSpec((total, width), lambda i: (0, 0)),
        ],
        out_specs=pl.BlockSpec((rows, width), lambda i: (i, 0)),
        compiler_params=pltpu.CompilerParams(vmem_limit_bytes=12 * MIB),
    )(slot, kv)


def local(
    tokens,
    segment_ids,
    routes,
    owners,
    gain_attn,
    w_query,
    w_kv,
    w_out,
    gain_moe,
    w_router,
    w_gate,
    w_up,
    w_down,
):
    seq_count = lax.axis_size("seq")
    ten_count = lax.axis_size("tensor")
    seq_rank = lax.axis_index("seq").astype(jnp.int32)
    ten_rank = lax.axis_index("tensor").astype(jnp.int32)
    rows, width = tokens.shape
    total = segment_ids.shape[0]
    w_out, w_gate, w_up, w_down = (
        pltpu.with_memory_space_constraint(w, pltpu.HBM) for w in (w_out, w_gate, w_up, w_down)
    )
    share = width // ten_count
    group = HEADS // KV_HEADS
    z = ten_rank // 2
    c = ten_rank - z * 2
    first = seq_rank * rows

    short_count = owners.shape[0] - 1
    labels = jnp.where(segment_ids < 0, short_count + 1, segment_ids)
    my_labels = lax.dynamic_slice_in_dim(labels, first, rows)
    seg_start = jnp.sum((labels[None, :] < my_labels[:, None]).astype(jnp.int32), axis=1)
    position = first + jnp.arange(rows, dtype=jnp.int32) - seg_start

    values = tokens.astype(F32)
    scale = lax.rsqrt(jnp.mean(values * values, axis=-1, keepdims=True) + EPS)
    normed = (values * scale * gain_attn).astype(BF16)
    half_dim = HEAD_DIM // 2
    freqs = THETA ** (-(jnp.arange(half_dim, dtype=F32) * 2.0) / HEAD_DIM)
    angles = position.astype(F32)[:, None] * freqs[None, :]
    cosine = jnp.cos(angles)
    sine = jnp.sin(angles)
    pairs = jnp.dot(normed, w_kv, preferred_element_type=F32)
    keys = rotate(pairs[:, :HEAD_DIM], cosine, sine).astype(BF16)
    kv_own = jnp.concatenate([keys, pairs[:, HEAD_DIM:].astype(BF16)], axis=1)
    queries = jnp.dot(normed, w_query, preferred_element_type=F32)
    q = jnp.concatenate(
        [
            rotate(queries[:, g * HEAD_DIM : (g + 1) * HEAD_DIM], cosine, sine).astype(BF16)
            for g in range(group)
        ],
        axis=0,
    )

    kv_all = lax.all_to_all(
        jnp.broadcast_to(kv_own[None], (seq_count,) + kv_own.shape), "seq", 0, 0, tiled=True
    ).reshape(total, kv_own.shape[1])

    g_sib, u_sib, d_sib = (send_core(w) for w in (w_gate, w_up, w_down))
    g_sib, u_sib, d_sib = (
        pltpu.with_memory_space_constraint(w, pltpu.HBM) for w in (g_sib, u_sib, d_sib)
    )
    weights = [w_gate, w_up, g_sib, u_sib, w_down, d_sib]

    ring = lax.rem(z + jnp.arange(NZ, dtype=jnp.int32), NZ) * 2
    other_c = 1 - c
    out_ids = jnp.concatenate([ring + c, ring + other_c])
    out_mine, out_sib = attend(
        out_ids, first.reshape(1), q, seg_start[:, None], kv_all, w_out, share
    )
    out_sib_r = send_core(out_sib)
    sums = [out_mine[d] + out_sib_r[d].astype(F32) for d in range(NZ)]
    attn_sum = sums[0]
    for d in (1, 3, 2):
        attn_sum = attn_sum + send_z(sums[d].astype(BF16), d).astype(F32)
    own_tokens = lax.dynamic_slice_in_dim(tokens, ten_rank * share, share, 1)
    residual = (own_tokens.astype(F32) + attn_sum).astype(BF16)

    sibling = send_core(residual)
    wide = jnp.where(
        c == 0,
        jnp.concatenate([residual, sibling], axis=1),
        jnp.concatenate([sibling, residual], axis=1),
    )

    slots = rows // 8
    holders = seq_count // EXPERTS
    expert_ids = jnp.arange(EXPERTS, dtype=jnp.int32)
    hit = (routes[:, 0:1] == expert_ids[None, :]) | (routes[:, 1:2] == expert_ids[None, :])
    index = jnp.arange(rows, dtype=jnp.int32)
    before = (index[:, None] > index[None, :]).astype(BF16)
    rank = jnp.dot(before, hit.astype(BF16), preferred_element_type=F32).astype(jnp.int32)
    slot_of = jnp.where(hit, rank, -1)
    slot_dup = jnp.repeat(slot_of.T, holders, axis=0)

    def pack(chunk):
        want = (2 * c + chunk) * slots + jnp.arange(slots, dtype=jnp.int32)
        return slot_dup[:, None, :] == want[None, :, None]

    picks = [pack(0), pack(1)]

    def exchange(flat):
        got = lax.all_to_all(
            flat.reshape(seq_count, slots, 2 * share), "seq", 0, 0, tiled=True
        )
        return got.reshape(seq_count * slots, 2 * share)

    def dispatch(pick):
        flat = pick.reshape(seq_count * slots, rows).astype(BF16)
        return exchange(jnp.dot(flat, wide, preferred_element_type=F32).astype(BF16))

    gain_wide = lax.dynamic_slice_in_dim(gain_moe, z * 2 * share, 2 * share)
    router = lax.dynamic_slice_in_dim(w_router, z * 2 * share, 2 * share)
    wide32 = wide.astype(F32)
    part = jnp.dot(
        wide32 * gain_wide, router, preferred_element_type=F32, precision=lax.Precision.HIGHEST
    )
    square = jnp.sum(wide32 * wide32, axis=1, keepdims=True)
    stats = jnp.concatenate([part, square, jnp.zeros((rows, 7), F32)], axis=1)
    stats = stats + lax.ppermute(stats, "tensor", [(t, t ^ 2) for t in range(ten_count)])
    stats = stats + lax.ppermute(stats, "tensor", [(t, t ^ 4) for t in range(ten_count)])
    logits = stats[:, :EXPERTS] * lax.rsqrt(stats[:, EXPERTS : EXPERTS + 1] / width + EPS)
    picked = routes[:, :, None] == expert_ids[None, None, :]
    chosen = jnp.sum(jnp.where(picked, logits[:, None, :], 0.0), axis=2)
    gates = jax.nn.softmax(chosen, axis=1)
    gate_of = jnp.sum(jnp.where(picked, gates[:, :, None], 0.0), axis=1)
    gate_dup = jnp.repeat(gate_of, holders, axis=1)

    gain_rows = gain_moe.reshape(NZ, 2 * share)
    ids = lax.rem(z + jnp.array([0, 3, 1, 2, 0, 1, 2, 3], jnp.int32), NZ)
    direct_outs = ((3, 3), (0, 0), (2, 2), (1, 1))
    ring_outs = ((3, 3), (2, 0), (0, 1), (1, 2))
    a_own = dispatch(picks[0])
    a_pieces = gather_ring(a_own)
    b_own = dispatch(picks[1])
    b_pieces = gather_direct(b_own)
    *a_out, g_held, u_held, d_held = ffn(ids, gain_rows, weights, a_pieces, direct_outs)
    held = [in_vmem(w) for w in (g_held, u_held, d_held)]
    b_out = ffn(ids, gain_rows, held, b_pieces, ring_outs)
    a_final = scatter_direct(*a_out)
    b_final = scatter_ring(*b_out)
    a_back = exchange(a_final)
    b_back = exchange(b_final)

    def combine(pick, back):
        weight = jnp.where(pick.transpose(2, 0, 1), gate_dup[:, :, None], 0.0)
        weight = weight.reshape(rows, seq_count * slots)
        high = weight.astype(BF16)
        low = (weight - high.astype(F32)).astype(BF16)
        return jnp.dot(high, back, preferred_element_type=F32) + jnp.dot(
            low, back, preferred_element_type=F32
        )

    mixture = combine(picks[0], a_back) + combine(picks[1], b_back)
    left, right = mixture[:, :share], mixture[:, share:]
    theirs = send_core(jnp.where(c == 0, right, left).astype(BF16))
    mine = jnp.where(c == 0, left, right)
    layer_out = (residual.astype(F32) + mine + theirs.astype(F32)).astype(BF16)

    owner_ext = jnp.concatenate([owners, jnp.full((1,), -1, jnp.int32)])
    label_ids = jnp.arange(short_count + 2, dtype=jnp.int32)
    owner_tok = jnp.sum(
        jnp.where(labels[:, None] == label_ids[None, :], owner_ext[None, :], 0), axis=1
    )
    held = (owner_tok == seq_rank).reshape(seq_count, rows)
    held_b = held.astype(BF16)
    inside = jnp.dot(held_b, before.T, preferred_element_type=F32)
    seq_index = jnp.arange(seq_count, dtype=jnp.int32)
    earlier = (seq_index[:, None] > seq_index[None, :]).astype(BF16)
    sizes = jnp.sum(held.astype(F32), axis=1).astype(BF16)
    ahead = jnp.dot(earlier, sizes[:, None], preferred_element_type=F32)
    slot = jnp.where(held, (inside + ahead).astype(jnp.int32), -1).reshape(1, total)
    cache = fill_cache(slot, kv_all)
    return layer_out, cache


def solution(mesh):
    return jax.shard_map(
        local,
        mesh=mesh,
        in_specs=(
            P("seq", None),
            P(),
            P("seq", None),
            P(),
            P(),
            P(None, "tensor"),
            P(None, "tensor"),
            P("tensor", None),
            P(),
            P(),
            P(None, ("seq", "tensor")),
            P(None, ("seq", "tensor")),
            P(("seq", "tensor"), None),
        ),
        out_specs=(P("seq", "tensor"), P("seq", "tensor")),
        check_vma=False,
    )
```

profile of v0, /device:TPU:33, one launch (start us, length us, event | category | flops | bytes accessed | tf_op | source)
XLA Modules:
  0.0 191.6 jit_solution(14464205220704459810)
XLA Ops:
  1.9 1.5 fusion
  3.4 1.7 fusion.11
  5.6 1.1 broadcast_in_dim.109
  6.6 6.8 %all-to-all-start = ((bf16[16,128,256]{2,1,0:T(8,128)(2,1)}), bf16[16,128,256]{2,1,0:T(8,128)(2,1)S(1)}, u32[]{:S(2)}, u32[]{:S(2)}) async-start(bf16[16,128,256]{2,1,0:T(8,128)(2,1)} %broadcast_in_dim.109), calls=%async_computation | async-start | bytes 2097152 | tf_op jit(solution)/shard_map/all_to_all | solution.py:365
  13.4 1.0 collective-permute-start.11
  15.0 2.9 %fusion.13 = f32[128,512]{1,0:T(8,128)S(1)} fusion(bf16[4096,512]{1,0:T(8,128)(2,1)} %param.19, bf16[128,4096]{1,0:T(8,128)(2,1)S(1)} %copy-done.8, f32[4096]{0:T(1024)S(1)} %copy-done.24, f32[128]{0:T(128)S(1)} %add_rsqrt_fusion), kind=kOutput, calls=%fused_computation.26 | convolution fusion | flops 538968064 | bytes 5521920 | tf_op jit(solution)/shard_map/dot_general | solution.py:356
  18.6 10.8 %all-to-all-done = bf16[16,128,256]{2,1,0:T(8,128)(2,1)S(1)} async-done(((bf16[16,128,256]{2,1,0:T(8,128)(2,1)}), bf16[16,128,256]{2,1,0:T(8,128)(2,1)S(1)}, u32[]{:S(2)}, u32[]{:S(2)}) %all-to-all-start) | async-done | bytes 1048608 | tf_op jit(solution)/shard_map/all_to_all | solution.py:365
  29.5 6.3 %shard_map.149 = (f32[4,128,512]{2,1,0:T(8,128)S(1)}, bf16[4,128,512]{2,1,0:T(8,128)(2,1)S(1)}) custom-call(s32[8]{0:T(128)S(1)} %pad_add_fusion.ids, s32[1]{0:T(128)} %bitcast.first_ref, bf16[512,128]{1,0:T(8,128)(2,1)S(1)} %maximum_maximum_fusion.q_ref, s32[128,1]{1,0:T(8,128)S(1)} %copy.19.start_ref, bf16[2048,256]{1,0:T(8,128)(2,1)S(1)} %bitcast.71, ...), custom_call_target="tpu_custom_call" | custom-call | tf_op jit(solution)/shard_map/pallas_call | solution.py:98
  35.7 2.7 %collective-permute-start = (bf16[4,128,512]{2,1,0:T(8,128)(2,1)S(1)}, bf16[4,128,512]{2,1,0:T(8,128)(2,1)}, u32[]{:S(2)}, u32[]{:S(2)}) collective-permute-start(bf16[4,128,512]{2,1,0:T(8,128)(2,1)S(1)} %get-tuple-element.20), channel_id=1, source_target_pairs={{0,1},{1,0},{2,3},{3,2},{4,5},{5,4},{6,7},{7,6},{8,9},{9,8},{10,11... | collective-permute-start | bytes 1572872 | tf_op jit(solution)/shard_map/ppermute | solution.py:43
  38.4 1.7 collective-permute-done
  40.1 1.2 fusion.22
  41.2 1.7 collective-permute-start.1
  43.6 2.4 %collective-permute-done.1 = bf16[128,512]{1,0:T(8,128)(2,1)S(1)} collective-permute-done((bf16[128,512]{1,0:T(8,128)(2,1)S(1)}, bf16[128,512]{1,0:T(8,128)(2,1)S(1)}, u32[]{:S(2)}, u32[]{:S(2)}) %collective-permute-start.1) | collective-permute-done | bytes 131104 | tf_op jit(solution)/shard_map/ppermute | solution.py:39
  46.0 2.7 %collective-permute-start.3 = (bf16[128,512]{1,0:T(8,128)(2,1)S(1)}, bf16[128,512]{1,0:T(8,128)(2,1)S(1)}, u32[]{:S(2)}, u32[]{:S(2)}) collective-permute-start(bf16[128,512]{1,0:T(8,128)(2,1)S(1)} %get-tuple-element.39), channel_id=1, source_target_pairs={{0,4},{1,5},{2,6},{3,7},{4,0},{5,1},{6,2},{7,3},{8,12},{9,13},{10,... | collective-permute-start | bytes 393224 | tf_op jit(solution)/shard_map/ppermute | solution.py:39
  48.7 2.6 %collective-permute-done.3 = bf16[128,512]{1,0:T(8,128)(2,1)S(1)} collective-permute-done((bf16[128,512]{1,0:T(8,128)(2,1)S(1)}, bf16[128,512]{1,0:T(8,128)(2,1)S(1)}, u32[]{:S(2)}, u32[]{:S(2)}) %collective-permute-start.3) | collective-permute-done | bytes 131104 | tf_op jit(solution)/shard_map/ppermute | solution.py:39
  51.3 1.1 fusion.18
  52.4 2.5 %collective-permute-start.4 = (bf16[128,512]{1,0:T(8,128)(2,1)S(1)}, bf16[128,512]{1,0:T(8,128)(2,1)S(1)}, u32[]{:S(2)}, u32[]{:S(2)}) collective-permute-start(bf16[128,512]{1,0:T(8,128)(2,1)S(1)} %fusion.18), channel_id=1, source_target_pairs={{0,1},{1,0},{2,3},{3,2},{4,5},{5,4},{6,7},{7,6},{8,9},{9,8},{10,11... | collective-permute-start | bytes 393224 | tf_op jit(solution)/shard_map/ppermute | solution.py:43
  56.1 13.6 %all_to_all.25 = bf16[16,16,1024]{2,1,0:T(8,128)(2,1)S(1)} all-to-all(bf16[16,16,1024]{2,1,0:T(8,128)(2,1)S(1)} %bitcast.82), channel_id=1, replica_groups=mesh['seq'=16,'tensor'=8] {'seq'}, dimensions={0} | all-to-all | bytes 1048576 | tf_op jit(solution)/shard_map/all_to_all | solution.py:413
  69.7 1.6 collective-permute-start.7
  71.9 1.1 convolution_convert_fusion
  73.0 3.6 %all-to-all-start.3 = ((bf16[16,16,1024]{2,1,0:T(8,128)(2,1)}), bf16[16,16,1024]{2,1,0:T(8,128)(2,1)S(1)}, u32[]{:S(2)}, u32[]{:S(2)}) async-start(bf16[16,16,1024]{2,1,0:T(8,128)(2,1)} %bitcast.81), calls=%async_computation.3 | async-start | bytes 1048576 | tf_op jit(solution)/shard_map/all_to_all | solution.py:413
  76.6 6.1 %collective-permute-done.7.below_ref.refs_1_ = bf16[256,1024]{1,0:T(8,128)(2,1)S(1)} collective-permute-done((bf16[256,1024]{1,0:T(8,128)(2,1)S(1)}, bf16[256,1024]{1,0:T(8,128)(2,1)S(1)}, u32[]{:S(2)}, u32[]{:S(2)}) %collective-permute-start.7) | collective-permute-done | bytes 524320 | tf_op jit(solution)/shard_map/ppermute | solution.py:39
  83.9 2.0 %collective-permute-start.10 = (bf16[128,1024]{1,0:T(8,128)(2,1)}, bf16[128,1024]{1,0:T(8,128)(2,1)S(1)}, u32[]{:S(2)}, u32[]{:S(2)}) collective-permute-start(bf16[128,1024]{1,0:T(8,128)(2,1)} %get-tuple-element.22), channel_id=1, source_target_pairs={{0,6},{1,7},{2,0},{3,1},{4,2},{5,3},{6,4},{7,5},{8,14},{9,15},{10,... | collective-permute-start | bytes 786440 | tf_op jit(solution)/shard_map/ppermute | solution.py:39
  85.9 1.3 dynamic_slice.14
  87.9 1.7 collective-permute-done.10.refs_4_
  89.5 2.5 %collective-permute-start.17 = (bf16[256,1024]{1,0:T(8,128)(2,1)S(1)}, bf16[256,1024]{1,0:T(8,128)(2,1)}, u32[]{:S(2)}, u32[]{:S(2)}) collective-permute-start(bf16[256,1024]{1,0:T(8,128)(2,1)S(1)} %bitcast.73), channel_id=1, source_target_pairs={{0,2},{1,3},{2,4},{3,5},{4,6},{5,7},{6,0},{7,1},{8,10},{9,11},{10,... | collective-permute-start | bytes 1572872 | tf_op jit(solution)/shard_map/ppermute | solution.py:39
  92.1 1.5 fusion.9
  93.6 1.1 fusion.10
  95.8 2.9 %collective-permute-start.5 = (f32[128,16]{0,1:T(8,128)S(1)}, f32[128,16]{0,1:T(8,128)S(1)}, u32[]{:S(2)}, u32[]{:S(2)}) collective-permute-start(f32[128,16]{0,1:T(8,128)S(1)} %maximum_maximum_fusion.1), channel_id=1, source_target_pairs={{0,2},{1,3},{2,0},{3,1},{4,6},{5,7},{6,4},{7,5},{8,10},{9,11},{10,... | collective-permute-start | bytes 24584 | tf_op jit(solution)/shard_map/ppermute | solution.py:430
  100.8 11.8 %shard_map.151 = (bf16[256,1024]{1,0:T(8,128)(2,1)S(1)}, bf16[256,1024]{1,0:T(8,128)(2,1)S(1)}, bf16[256,1024]{1,0:T(8,128)(2,1)S(1)}, bf16[256,1024]{1,0:T(8,12...) custom-call(s32[8]{0:T(128)S(1)} %compare_select_fusion.1.ids, ...), custom_call_target="tpu_custom_call" | custom-call | tf_op jit(solution)/shard_map/pallas_call | solution.py:191
  113.3 1.5 collective-permute-start.15
  114.7 1.8 collective-permute-start.16
  116.6 1.4 collective-permute-start.6
  118.1 9.8 %shard_map.153 = (bf16[256,1024]{1,0:T(8,128)(2,1)}, bf16[256,1024]{1,0:T(8,128)(2,1)}, bf16[256,1024]{1,0:T(8,128)(2,1)S(1)}, bf16[256,1024]{1,0:T(8,128)(2,1)S(1)}) custom-call(s32[8]{0:T(128)S(1)} %compare_select_fusion.1.ids, f32[4,1024]{1,0:T(4,128)S(1)} %reshape.172.gain_ref, bf16[256,1024]{1,0:T(8,128)(2,1)S(1)} %bitcast.76, ...), custom_call_target="tpu_custom_call" | custom-call | tf_op jit(solution)/shard_map/pallas_call | solution.py:191
  129.5 10.9 %collective-permute-done.6 = f32[128,16]{0,1:T(8,128)S(1)} collective-permute-done((f32[128,16]{0,1:T(8,128)S(1)}, f32[128,16]{0,1:T(8,128)S(1)}, u32[]{:S(2)}, u32[]{:S(2)}) %collective-permute-start.6) | collective-permute-done | bytes 8224 | tf_op jit(solution)/shard_map/ppermute | solution.py:431
  140.8 2.1 %shard_map.152 = bf16[256,1024]{1,0:T(8,128)(2,1)} custom-call(bf16[256,1024]{1,0:T(8,128)(2,1)} %copy-done.2, bf16[256,1024]{1,0:T(8,128)(2,1)S(1)} %collective-permute-done.14.refs_1_, bf16[256,1024]{1,0:T(8,128)(2,1)S(1)} %collective-permute-done.15.refs_2_, bf16[256,1024]{1,0:T(8,128)(2,1)S(1)} %collective-permute-done.16.refs_3_), custom_call_target="tpu_custom_call" | custom-call | tf_op jit(solution)/shard_map/pallas_call | solution.py:251
  143.0 6.0 %all-to-all-start.2 = ((bf16[16,16,1024]{2,1,0:T(8,128)(2,1)}), bf16[16,16,1024]{2,1,0:T(8,128)(2,1)S(1)}, u32[]{:S(2)}, u32[]{:S(2)}) async-start(bf16[16,16,1024]{2,1,0:T(8,128)(2,1)} %bitcast.17), calls=%async_computation.2 | async-start | bytes 1048576 | tf_op jit(solution)/shard_map/all_to_all | solution.py:413
  149.0 1.4 collective-permute-done.20.below_ref
  150.8 1.2 shard_map.154
  152.0 2.4 %collective-permute-start.22 = (bf16[128,1024]{1,0:T(8,128)(2,1)S(1)}, bf16[128,1024]{1,0:T(8,128)(2,1)S(1)}, u32[]{:S(2)}, u32[]{:S(2)}) collective-permute-start(bf16[128,1024]{1,0:T(8,128)(2,1)S(1)} %get-tuple-element.34), channel_id=1, source_target_pairs={{0,2},{1,3},{2,4},{3,5},{4,6},{5,7},{6,0},{7,1},{8,10},{9,11},{10,... | collective-permute-start | bytes 786440 | tf_op jit(solution)/shard_map/ppermute | solution.py:39
  154.4 0.9 collective-permute-start.23
  155.4 3.9 %collective-permute-done.22.low_ref = bf16[128,1024]{1,0:T(8,128)(2,1)S(1)} collective-permute-done((bf16[128,1024]{1,0:T(8,128)(2,1)S(1)}, bf16[128,1024]{1,0:T(8,128)(2,1)S(1)}, u32[]{:S(2)}, u32[]{:S(2)}) %collective-permute-start.22) | collective-permute-done | bytes 262176 | tf_op jit(solution)/shard_map/ppermute | solution.py:39
  160.0 2.2 %shard_map.155 = bf16[256,1024]{1,0:T(8,128)(2,1)} custom-call(bf16[256,1024]{1,0:T(8,128)(2,1)} %copy-done.3, bf16[256,1024]{1,0:T(8,128)(2,1)S(1)} %collective-permute-done.20.below_ref, bf16[256,1024]{1,0:T(8,128)(2,1)S(1)} %collective-permute-done.21.above_ref, bf16[128,1024]{1,0:T(8,128)(2,1)} %copy-done.11, ...), custom_call_target="tpu_custom_call" | custom-call | tf_op jit(solution)/shard_map/pallas_call | solution.py:251
  162.2 4.8 %all-to-all-start.4 = ((bf16[16,16,1024]{2,1,0:T(8,128)(2,1)}), bf16[16,16,1024]{2,1,0:T(8,128)(2,1)S(1)}, u32[]{:S(2)}, u32[]{:S(2)}) async-start(bf16[16,16,1024]{2,1,0:T(8,128)(2,1)} %bitcast.22), calls=%async_computation.4 | async-start | bytes 1048576 | tf_op jit(solution)/shard_map/all_to_all | solution.py:413
  167.1 1.1 convolution_bitcast_fusion.2
  168.2 7.8 %all-to-all-done.4 = bf16[16,16,1024]{2,1,0:T(8,128)(2,1)S(1)} async-done(((bf16[16,16,1024]{2,1,0:T(8,128)(2,1)}), bf16[16,16,1024]{2,1,0:T(8,128)(2,1)S(1)}, u32[]{:S(2)}, u32[]{:S(2)}) %all-to-all-start.4) | async-done | bytes 524320 | tf_op jit(solution)/shard_map/all_to_all | solution.py:413
  177.6 8.3 %collective-permute-start.24 = (bf16[128,512]{1,0:T(8,128)(2,1)S(1)}, bf16[128,512]{1,0:T(8,128)(2,1)S(1)}, u32[]{:S(2)}, u32[]{:S(2)}) collective-permute-start(bf16[128,512]{1,0:T(8,128)(2,1)S(1)} %select_convert_fusion), channel_id=1, source_target_pairs={{0,1},{1,0},{2,3},{3,2},{4,5},{5,4},{6,7},{7,6},{8,9},{9,8},{10,11... | collective-permute-start | bytes 393224 | tf_op jit(solution)/shard_map/ppermute | solution.py:43
  186.0 4.9 %shard_map.156 = bf16[2048,256]{1,0:T(8,128)(2,1)} custom-call(s32[1,2048]{1,0:T(1,128)S(1)} %bitcast.80, bf16[2048,256]{1,0:T(8,128)(2,1)S(1)} %bitcast.72), custom_call_target="tpu_custom_call" | custom-call | tf_op jit(solution)/shard_map/pallas_call | solution.py:296
  (132 shorter events, 16.7 us)
Async XLA Ops:
  5.1 9.8 %copy-start.8 = (bf16[128,4096]{1,0:T(8,128)(2,1)S(1)}, bf16[128,4096]{1,0:T(8,128)(2,1)}, u32[]{:S(2)}) copy-start(bf16[128,4096]{1,0:T(8,128)(2,1)} %param.14) | copy-start | bytes 3145732
  5.1 9.8 %copy-start.24 = (f32[4096]{0:T(1024)S(1)}, f32[4096]{0:T(1024)}, u32[]{:S(2)}) copy-start(f32[4096]{0:T(1024)} %param.18) | copy-start | bytes 49156
  6.6 22.8 %all-to-all-start = ((bf16[16,128,256]{2,1,0:T(8,128)(2,1)}), bf16[16,128,256]{2,1,0:T(8,128)(2,1)S(1)}, u32[]{:S(2)}, u32[]{:S(2)}) async-start(bf16[16,128,256]{2,1,0:T(8,128)(2,1)} %broadcast_in_dim.109), calls=%async_computation | async-start | bytes 2097152 | tf_op jit(solution)/shard_map/all_to_all | solution.py:365
  13.4 82.4 %collective-permute-start.11 = (bf16[4096,512]{1,0:T(8,128)(2,1)}, bf16[4096,512]{1,0:T(8,128)(2,1)}, u32[]{:S(2)}, u32[]{:S(2)}) collective-permute-start(bf16[4096,512]{1,0:T(8,128)(2,1)} %refs_5_.1), channel_id=1, source_target_pairs={{0,1},{1,0},{2,3},{3,2},{4,5},{5,4},{6,7},{7,6},{8,9},{9,8},{10,11... | collective-permute-start | bytes 12582920 | tf_op jit(solution)/shard_map/ppermute | solution.py:43
  14.4 84.2 %collective-permute-start.12 = (bf16[4096,512]{1,0:T(8,128)(2,1)}, bf16[4096,512]{1,0:T(8,128)(2,1)}, u32[]{:S(2)}, u32[]{:S(2)}) collective-permute-start(bf16[4096,512]{1,0:T(8,128)(2,1)} %refs_6_.1), channel_id=1, source_target_pairs={{0,1},{1,0},{2,3},{3,2},{4,5},{5,4},{6,7},{7,6},{8,9},{9,8},{10,11... | collective-permute-start | bytes 12582920 | tf_op jit(solution)/shard_map/ppermute | solution.py:43
  14.5 86.2 %collective-permute-start.13 = (bf16[512,4096]{1,0:T(8,128)(2,1)}, bf16[512,4096]{1,0:T(8,128)(2,1)}, u32[]{:S(2)}, u32[]{:S(2)}) collective-permute-start(bf16[512,4096]{1,0:T(8,128)(2,1)} %refs_9_.1), channel_id=1, source_target_pairs={{0,1},{1,0},{2,3},{3,2},{4,5},{5,4},{6,7},{7,6},{8,9},{9,8},{10,11... | collective-permute-start | bytes 12582920 | tf_op jit(solution)/shard_map/ppermute | solution.py:43
  29.5 19.2 %copy-start.15 = (s32[128,2]{0,1:T(2,128)S(1)}, s32[128,2]{0,1:T(2,128)}, u32[]{:S(2)}) copy-start(s32[128,2]{0,1:T(2,128)} %param.16) | copy-start | bytes 3076
  35.7 4.3 %collective-permute-start = (bf16[4,128,512]{2,1,0:T(8,128)(2,1)S(1)}, bf16[4,128,512]{2,1,0:T(8,128)(2,1)}, u32[]{:S(2)}, u32[]{:S(2)}) collective-permute-start(bf16[4,128,512]{2,1,0:T(8,128)(2,1)S(1)} %get-tuple-element.20), channel_id=1, source_target_pairs={{0,1},{1,0},{2,3},{3,2},{4,5},{5,4},{6,7},{7,6},{8,9},{9,8},{10,11... | collective-permute-start | bytes 1572872 | tf_op jit(solution)/shard_map/ppermute | solution.py:43
  41.2 4.8 %collective-permute-start.1 = (bf16[128,512]{1,0:T(8,128)(2,1)S(1)}, bf16[128,512]{1,0:T(8,128)(2,1)S(1)}, u32[]{:S(2)}, u32[]{:S(2)}) collective-permute-start(bf16[128,512]{1,0:T(8,128)(2,1)S(1)} %get-tuple-element.38), channel_id=1, source_target_pairs={{0,2},{1,3},{2,4},{3,5},{4,6},{5,7},{6,0},{7,1},{8,10},{9,11},{10,... | collective-permute-start | bytes 393224 | tf_op jit(solution)/shard_map/ppermute | solution.py:39
  43.5 5.1 %collective-permute-start.2 = (bf16[128,512]{1,0:T(8,128)(2,1)S(1)}, bf16[128,512]{1,0:T(8,128)(2,1)S(1)}, u32[]{:S(2)}, u32[]{:S(2)}) collective-permute-start(bf16[128,512]{1,0:T(8,128)(2,1)S(1)} %get-tuple-element.40), channel_id=1, source_target_pairs={{0,6},{1,7},{2,0},{3,1},{4,2},{5,3},{6,4},{7,5},{8,14},{9,15},{10,... | collective-permute-start | bytes 393224 | tf_op jit(solution)/shard_map/ppermute | solution.py:39
  46.0 5.3 %collective-permute-start.3 = (bf16[128,512]{1,0:T(8,128)(2,1)S(1)}, bf16[128,512]{1,0:T(8,128)(2,1)S(1)}, u32[]{:S(2)}, u32[]{:S(2)}) collective-permute-start(bf16[128,512]{1,0:T(8,128)(2,1)S(1)} %get-tuple-element.39), channel_id=1, source_target_pairs={{0,4},{1,5},{2,6},{3,7},{4,0},{5,1},{6,2},{7,3},{8,12},{9,13},{10,... | collective-permute-start | bytes 393224 | tf_op jit(solution)/shard_map/ppermute | solution.py:39
  52.4 41.2 %copy-start.9 = (bf16[128,512]{1,0:T(8,128)(2,1)}, bf16[128,512]{1,0:T(8,128)(2,1)S(1)}, u32[]{:S(2)}) copy-start(bf16[128,512]{1,0:T(8,128)(2,1)S(1)} %fusion.18) | copy-start | bytes 393220
  52.4 3.4 %collective-permute-start.4 = (bf16[128,512]{1,0:T(8,128)(2,1)S(1)}, bf16[128,512]{1,0:T(8,128)(2,1)S(1)}, u32[]{:S(2)}, u32[]{:S(2)}) collective-permute-start(bf16[128,512]{1,0:T(8,128)(2,1)S(1)} %fusion.18), channel_id=1, source_target_pairs={{0,1},{1,0},{2,3},{3,2},{4,5},{5,4},{6,7},{7,6},{8,9},{9,8},{10,11... | collective-permute-start | bytes 393224 | tf_op jit(solution)/shard_map/ppermute | solution.py:43
  55.8 16.0 %copy-start.12 = (bf16[128,512]{1,0:T(8,128)(2,1)}, bf16[128,512]{1,0:T(8,128)(2,1)S(1)}, u32[]{:S(2)}) copy-start(bf16[128,512]{1,0:T(8,128)(2,1)S(1)} %collective-permute-done.4) | copy-start | bytes 393220
  69.7 12.9 %collective-permute-start.7 = (bf16[256,1024]{1,0:T(8,128)(2,1)S(1)}, bf16[256,1024]{1,0:T(8,128)(2,1)S(1)}, u32[]{:S(2)}, u32[]{:S(2)}) collective-permute-start(bf16[256,1024]{1,0:T(8,128)(2,1)S(1)} %bitcast.77), channel_id=1, source_target_pairs={{0,2},{1,3},{2,4},{3,5},{4,6},{5,7},{6,0},{7,1},{8,10},{9,11},{10,... | collective-permute-start | bytes 1572872 | tf_op jit(solution)/shard_map/ppermute | solution.py:39
  71.4 11.7 %collective-permute-start.8 = (bf16[256,1024]{1,0:T(8,128)(2,1)S(1)}, bf16[256,1024]{1,0:T(8,128)(2,1)S(1)}, u32[]{:S(2)}, u32[]{:S(2)}) collective-permute-start(bf16[256,1024]{1,0:T(8,128)(2,1)S(1)} %bitcast.78), channel_id=1, source_target_pairs={{0,6},{1,7},{2,0},{3,1},{4,2},{5,3},{6,4},{7,5},{8,14},{9,15},{10,... | collective-permute-start | bytes 1572872 | tf_op jit(solution)/shard_map/ppermute | solution.py:39
  73.0 14.9 %all-to-all-start.3 = ((bf16[16,16,1024]{2,1,0:T(8,128)(2,1)}), bf16[16,16,1024]{2,1,0:T(8,128)(2,1)S(1)}, u32[]{:S(2)}, u32[]{:S(2)}) async-start(bf16[16,16,1024]{2,1,0:T(8,128)(2,1)} %bitcast.81), calls=%async_computation.3 | async-start | bytes 1048576 | tf_op jit(solution)/shard_map/all_to_all | solution.py:413
  83.9 5.6 %collective-permute-start.10 = (bf16[128,1024]{1,0:T(8,128)(2,1)}, bf16[128,1024]{1,0:T(8,128)(2,1)S(1)}, u32[]{:S(2)}, u32[]{:S(2)}) collective-permute-start(bf16[128,1024]{1,0:T(8,128)(2,1)} %get-tuple-element.22), channel_id=1, source_target_pairs={{0,6},{1,7},{2,0},{3,1},{4,2},{5,3},{6,4},{7,5},{8,14},{9,15},{10,... | collective-permute-start | bytes 786440 | tf_op jit(solution)/shard_map/ppermute | solution.py:39
  85.9 8.9 %collective-permute-start.9 = (bf16[128,1024]{1,0:T(8,128)(2,1)}, bf16[128,1024]{1,0:T(8,128)(2,1)}, u32[]{:S(2)}, u32[]{:S(2)}) collective-permute-start(bf16[128,1024]{1,0:T(8,128)(2,1)} %get-tuple-element.21), channel_id=1, source_target_pairs={{0,2},{1,3},{2,4},{3,5},{4,6},{5,7},{6,0},{7,1},{8,10},{9,11},{10,... | collective-permute-start | bytes 786440 | tf_op jit(solution)/shard_map/ppermute | solution.py:39
  89.5 25.2 %collective-permute-start.17 = (bf16[256,1024]{1,0:T(8,128)(2,1)S(1)}, bf16[256,1024]{1,0:T(8,128)(2,1)}, u32[]{:S(2)}, u32[]{:S(2)}) collective-permute-start(bf16[256,1024]{1,0:T(8,128)(2,1)S(1)} %bitcast.73), channel_id=1, source_target_pairs={{0,2},{1,3},{2,4},{3,5},{4,6},{5,7},{6,0},{7,1},{8,10},{9,11},{10,... | collective-permute-start | bytes 1572872 | tf_op jit(solution)/shard_map/ppermute | solution.py:39
  93.6 5.8 %copy-start.13 = (f32[128,8]{0,1:T(8,128)}, f32[128,8]{0,1:T(8,128)S(1)}, u32[]{:S(2)}) copy-start(f32[128,8]{0,1:T(8,128)S(1)} %fusion.9) | copy-start | bytes 12292
  94.7 4.6 %copy-start.21 = (f32[128]{0:T(128)}, f32[128]{0:T(128)S(1)}, u32[]{:S(2)}) copy-start(f32[128]{0:T(128)S(1)} %fusion.10) | copy-start | bytes 1540
  94.8 21.8 %collective-permute-start.18 = (bf16[256,1024]{1,0:T(8,128)(2,1)S(1)}, bf16[256,1024]{1,0:T(8,128)(2,1)}, u32[]{:S(2)}, u32[]{:S(2)}) collective-permute-start(bf16[256,1024]{1,0:T(8,128)(2,1)S(1)} %bitcast.74), channel_id=1, source_target_pairs={{0,6},{1,7},{2,0},{3,1},{4,2},{5,3},{6,4},{7,5},{8,14},{9,15},{10,... | collective-permute-start | bytes 1572872 | tf_op jit(solution)/shard_map/ppermute | solution.py:39
  95.8 17.5 %collective-permute-start.5 = (f32[128,16]{0,1:T(8,128)S(1)}, f32[128,16]{0,1:T(8,128)S(1)}, u32[]{:S(2)}, u32[]{:S(2)}) collective-permute-start(f32[128,16]{0,1:T(8,128)S(1)} %maximum_maximum_fusion.1), channel_id=1, source_target_pairs={{0,2},{1,3},{2,0},{3,1},{4,6},{5,7},{6,4},{7,5},{8,10},{9,11},{10,... | collective-permute-start | bytes 24584 | tf_op jit(solution)/shard_map/ppermute | solution.py:430
  98.7 19.4 %collective-permute-start.19 = (bf16[256,1024]{1,0:T(8,128)(2,1)S(1)}, bf16[256,1024]{1,0:T(8,128)(2,1)}, u32[]{:S(2)}, u32[]{:S(2)}) collective-permute-start(bf16[256,1024]{1,0:T(8,128)(2,1)S(1)} %bitcast.75), channel_id=1, source_target_pairs={{0,4},{1,5},{2,6},{3,7},{4,0},{5,1},{6,2},{7,3},{8,12},{9,13},{10,... | collective-permute-start | bytes 1572872 | tf_op jit(solution)/shard_map/ppermute | solution.py:39
  100.7 15.8 %copy-start.14 = (f32[128,8]{0,1:T(8,128)S(1)}, f32[128,8]{0,1:T(8,128)}, u32[]{:S(2)}) copy-start(f32[128,8]{0,1:T(8,128)} %copy-done.13) | copy-start | bytes 12292
  100.8 15.8 %copy-start.22 = (f32[128]{0:T(128)S(1)}, f32[128]{0:T(128)}, u32[]{:S(2)}) copy-start(f32[128]{0:T(128)} %copy-done.21) | copy-start | bytes 1540
  100.8 15.8 %copy-start.23 = (f32[16]{0:T(128)S(1)}, f32[16]{0:T(128)}, u32[]{:S(2)}) copy-start(f32[16]{0:T(128)} %pad.4.clone) | copy-start | bytes 196
  100.8 17.3 %copy-start.25 = (s32[15]{0:T(128)S(1)}, s32[15]{0:T(128)}, u32[]{:S(2)}) copy-start(s32[15]{0:T(128)} %param.17) | copy-start | bytes 184
  112.6 15.3 %copy-start.2 = (bf16[256,1024]{1,0:T(8,128)(2,1)}, bf16[256,1024]{1,0:T(8,128)(2,1)S(1)}, u32[]{:S(2)}) copy-start(bf16[256,1024]{1,0:T(8,128)(2,1)S(1)} %get-tuple-element.23.refs_0_) | copy-start | bytes 1572868
  112.6 28.2 %collective-permute-start.14 = (bf16[256,1024]{1,0:T(8,128)(2,1)S(1)}, bf16[256,1024]{1,0:T(8,128)(2,1)S(1)}, u32[]{:S(2)}, u32[]{:S(2)}) collective-permute-start(bf16[256,1024]{1,0:T(8,128)(2,1)S(1)} %get-tuple-element.24), channel_id=1, source_target_pairs={{0,2},{1,3},{2,4},{3,5},{4,6},{5,7},{6,0},{7,1},{8,10},{9,11},{10,... | collective-permute-start | bytes 1572872 | tf_op jit(solution)/shard_map/ppermute | solution.py:39
  113.3 27.5 %collective-permute-start.15 = (bf16[256,1024]{1,0:T(8,128)(2,1)S(1)}, bf16[256,1024]{1,0:T(8,128)(2,1)S(1)}, u32[]{:S(2)}, u32[]{:S(2)}) collective-permute-start(bf16[256,1024]{1,0:T(8,128)(2,1)S(1)} %get-tuple-element.25), channel_id=1, source_target_pairs={{0,6},{1,7},{2,0},{3,1},{4,2},{5,3},{6,4},{7,5},{8,14},{9,15},{10,... | collective-permute-start | bytes 1572872 | tf_op jit(solution)/shard_map/ppermute | solution.py:39
  114.7 26.1 %collective-permute-start.16 = (bf16[256,1024]{1,0:T(8,128)(2,1)S(1)}, bf16[256,1024]{1,0:T(8,128)(2,1)S(1)}, u32[]{:S(2)}, u32[]{:S(2)}) collective-permute-start(bf16[256,1024]{1,0:T(8,128)(2,1)S(1)} %get-tuple-element.26), channel_id=1, source_target_pairs={{0,4},{1,5},{2,6},{3,7},{4,0},{5,1},{6,2},{7,3},{8,12},{9,13},{10,... | collective-permute-start | bytes 1572872 | tf_op jit(solution)/shard_map/ppermute | solution.py:39
  116.6 23.9 %collective-permute-start.6 = (f32[128,16]{0,1:T(8,128)S(1)}, f32[128,16]{0,1:T(8,128)S(1)}, u32[]{:S(2)}, u32[]{:S(2)}) collective-permute-start(f32[128,16]{0,1:T(8,128)S(1)} %fusion.104), channel_id=1, source_target_pairs={{0,4},{1,5},{2,6},{3,7},{4,0},{5,1},{6,2},{7,3},{8,12},{9,13},{10,... | collective-permute-start | bytes 24584 | tf_op jit(solution)/shard_map/ppermute | solution.py:431
  128.7 14.3 %copy-start.4 = (bf16[256,1024]{1,0:T(8,128)(2,1)}, bf16[256,1024]{1,0:T(8,128)(2,1)S(1)}, u32[]{:S(2)}) copy-start(bf16[256,1024]{1,0:T(8,128)(2,1)S(1)} %get-tuple-element.33.relay_ref) | copy-start | bytes 1572868
  128.7 21.7 %collective-permute-start.20 = (bf16[256,1024]{1,0:T(8,128)(2,1)}, bf16[256,1024]{1,0:T(8,128)(2,1)S(1)}, u32[]{:S(2)}, u32[]{:S(2)}) collective-permute-start(bf16[256,1024]{1,0:T(8,128)(2,1)} %get-tuple-element.31), channel_id=1, source_target_pairs={{0,2},{1,3},{2,4},{3,5},{4,6},{5,7},{6,0},{7,1},{8,10},{9,11},{10,... | collective-permute-start | bytes 1572872 | tf_op jit(solution)/shard_map/ppermute | solution.py:39
  140.5 10.4 %collective-permute-start.21 = (bf16[256,1024]{1,0:T(8,128)(2,1)}, bf16[256,1024]{1,0:T(8,128)(2,1)S(1)}, u32[]{:S(2)}, u32[]{:S(2)}) collective-permute-start(bf16[256,1024]{1,0:T(8,128)(2,1)} %get-tuple-element.32), channel_id=1, source_target_pairs={{0,6},{1,7},{2,0},{3,1},{4,2},{5,3},{6,4},{7,5},{8,14},{9,15},{10,... | collective-permute-start | bytes 1572872 | tf_op jit(solution)/shard_map/ppermute | solution.py:39
  140.8 14.5 %copy-start.16 = (s32[128,2]{0,1:T(2,128)S(1)}, s32[128,2]{0,1:T(2,128)}, u32[]{:S(2)}) copy-start(s32[128,2]{0,1:T(2,128)} %param.16) | copy-start | bytes 3076
  143.0 19.2 %all-to-all-start.2 = ((bf16[16,16,1024]{2,1,0:T(8,128)(2,1)}), bf16[16,16,1024]{2,1,0:T(8,128)(2,1)S(1)}, u32[]{:S(2)}, u32[]{:S(2)}) async-start(bf16[16,16,1024]{2,1,0:T(8,128)(2,1)} %bitcast.17), calls=%async_computation.2 | async-start | bytes 1048576 | tf_op jit(solution)/shard_map/all_to_all | solution.py:413
  152.0 15.1 %copy-start.20 = (s32[16]{0:T(128)S(1)}, s32[16]{0:T(128)}, u32[]{:S(2)}) copy-start(s32[16]{0:T(128)} %copy-done.19) | copy-start | bytes 196
  152.0 7.3 %collective-permute-start.22 = (bf16[128,1024]{1,0:T(8,128)(2,1)S(1)}, bf16[128,1024]{1,0:T(8,128)(2,1)S(1)}, u32[]{:S(2)}, u32[]{:S(2)}) collective-permute-start(bf16[128,1024]{1,0:T(8,128)(2,1)S(1)} %get-tuple-element.34), channel_id=1, source_target_pairs={{0,2},{1,3},{2,4},{3,5},{4,6},{5,7},{6,0},{7,1},{8,10},{9,11},{10,... | collective-permute-start | bytes 786440 | tf_op jit(solution)/shard_map/ppermute | solution.py:39
  154.4 5.5 %collective-permute-start.23 = (bf16[128,1024]{1,0:T(8,128)(2,1)S(1)}, bf16[128,1024]{1,0:T(8,128)(2,1)}, u32[]{:S(2)}, u32[]{:S(2)}) collective-permute-start(bf16[128,1024]{1,0:T(8,128)(2,1)S(1)} %get-tuple-element.35), channel_id=1, source_target_pairs={{0,6},{1,7},{2,0},{3,1},{4,2},{5,3},{6,4},{7,5},{8,14},{9,15},{10,... | collective-permute-start | bytes 786440 | tf_op jit(solution)/shard_map/ppermute | solution.py:39
  160.0 16.0 %copy-start.18 = (s32[16]{0:T(128)S(1)}, s32[16]{0:T(128)}, u32[]{:S(2)}) copy-start(s32[16]{0:T(128)} %copy-done.17) | copy-start | bytes 196
  162.2 4.9 %copy-start.5 = (bf16[16,16,1024]{2,1,0:T(8,128)(2,1)}, bf16[16,16,1024]{2,1,0:T(8,128)(2,1)S(1)}, u32[]{:S(2)}) copy-start(bf16[16,16,1024]{2,1,0:T(8,128)(2,1)S(1)} %all-to-all-done.2) | copy-start | bytes 1572868
  162.2 13.8 %all-to-all-start.4 = ((bf16[16,16,1024]{2,1,0:T(8,128)(2,1)}), bf16[16,16,1024]{2,1,0:T(8,128)(2,1)S(1)}, u32[]{:S(2)}, u32[]{:S(2)}) async-start(bf16[16,16,1024]{2,1,0:T(8,128)(2,1)} %bitcast.22), calls=%async_computation.4 | async-start | bytes 1048576 | tf_op jit(solution)/shard_map/all_to_all | solution.py:413
  177.2 13.7 %copy-start.10 = (bf16[128,512]{1,0:T(8,128)(2,1)S(1)}, bf16[128,512]{1,0:T(8,128)(2,1)}, u32[]{:S(2)}) copy-start(bf16[128,512]{1,0:T(8,128)(2,1)} %copy-done.9) | copy-start | bytes 393220
  177.2 14.4 %copy-start.1 = (bf16[4096,256]{1,0:T(8,128)(2,1)S(1)}, bf16[4096,256]{1,0:T(8,128)(2,1)}, u32[]{:S(2)}) copy-start(bf16[4096,256]{1,0:T(8,128)(2,1)} %param.20) | copy-start | bytes 6291460
  177.6 13.3 %collective-permute-start.24 = (bf16[128,512]{1,0:T(8,128)(2,1)S(1)}, bf16[128,512]{1,0:T(8,128)(2,1)S(1)}, u32[]{:S(2)}, u32[]{:S(2)}) collective-permute-start(bf16[128,512]{1,0:T(8,128)(2,1)S(1)} %select_convert_fusion), channel_id=1, source_target_pairs={{0,1},{1,0},{2,3},{3,2},{4,5},{5,4},{6,7},{7,6},{8,9},{9,8},{10,11... | collective-permute-start | bytes 393224 | tf_op jit(solution)/shard_map/ppermute | solution.py:43
  (7 other events, 7.6 us)
where the time goes:
time: 194 us; the launch traced here: 192 us
  starting transfers between devices  60.6 us (31%)
  waiting for transfers between devices  51.4 us (26%)
  Pallas kernels  39 us (20%)
  blocking collectives  13.6 us (7%)
  matrix products  10.2 us (5%)
  other arithmetic  9.76 us (5%)
  local copies, waits for them, and re-layouts  6.09 us (3%)
    pallas_call x2, Pallas kernels, ffn(): pl.pallas_call(functools.partial(ffn_kernel, len(pieces), targets), out_s...  21.6 us
    ppermute x17, starting transfers between devices, send_z(): return lax.ppermute(value, 'tensor', z_perm(step))  20.1 us
    ppermute x17, waiting for transfers between devices, send_z(): return lax.ppermute(value, 'tensor', z_perm(step))  19.6 us
    ppermute x6, starting transfers between devices, send_core(): return lax.ppermute(value, 'tensor', core_perm())  15 us
    all_to_all x3, starting transfers between devices, exchange(): lax.all_to_all(flat.reshape(seq_count, slots, 2 * share), 'seq', 0, 0, ti...  14.4 us
    all_to_all x1, blocking collectives, exchange(): lax.all_to_all(flat.reshape(seq_count, slots, 2 * share), 'seq', 0, 0, ti...  13.6 us
    ppermute x1, waiting for transfers between devices, local(): lax.ppermute(stats, 'tensor', [(t, t ^ 4) for t in range(ten_count)])  10.9 us
    all_to_all x1, waiting for transfers between devices, local(): lax.all_to_all(jnp.broadcast_to(kv_own[None], (seq_count,) + kv_own.shape...  10.8 us
  transfers between devices with their start and end apart: 29, of which 14 were waited for; matrix products, arithmetic and copies ran while one was open for 9% of the time, Pallas kernels for 20%

commit v1 on v0

--- a/solution.py
+++ b/solution.py
@@ -108,12 +108,16 @@
     )(ids, first, q, start, kv, w_out)
 
 
-def ffn_kernel(count, pieces_to_outs, ids, gain_ref, *refs):
+def hidden_kernel(count, ids, gain_ref, *refs):
     pieces, refs = refs[:count], refs[count:]
     copies = []
-    if len(refs) > 9:
-        sources, outs, held, (xs_ref, act_ref, sems) = refs[:6], refs[6:10], refs[10:13], refs[13:]
-        gate_ref, up_ref, down_ref = held
+    if len(refs) > 4:
+        sources, act_ref, (gate_ref, up_ref, down_ref), (xs_ref, sems) = (
+            refs[:6],
+            refs[6],
+            refs[7:10],
+            refs[10:],
+        )
         places = [gate_ref.at[0], up_ref.at[0], gate_ref.at[1], up_ref.at[1]]
         places += [down_ref.at[0], down_ref.at[1]]
         copies = [
@@ -121,25 +125,16 @@
             for i, (source, ref) in enumerate(zip(sources, places, strict=True))
         ]
     else:
-        gate_ref, up_ref, down_ref = refs[:3]
-        outs, (xs_ref, act_ref) = refs[3:7], refs[7:]
+        gate_ref, up_ref, act_ref, xs_ref = refs
     for copy in copies[:3]:
         copy.start()
-
-    def arrived(i):
-        if copies:
-            copies[i].wait()
-            if i + 3 < len(copies):
-                copies[i + 3].start()
-
     rows, share = pieces[0].shape
     half = rows // 2
     width = gate_ref.shape[1]
     tile = 32
 
     for side in range(2):
-        chosen = [(pieces[k], 0, k) for k in range(3)]
-        chosen += [(pieces[3 + side], side * half, 3) if len(pieces) > 4 else (pieces[3], 0, 3)]
+        chosen = [(pieces[k], 0, k) for k in range(3)] + [(pieces[3 + side], side * half, 3)]
 
         def norm(i, carry):
             at_row = pl.multiple_of(side * half + i * tile, tile)
@@ -159,43 +154,68 @@
 
         lax.fori_loop(0, half // tile, norm, 0)
 
+    def arrived(i):
+        if copies:
+            copies[i].wait()
+            if i + 3 < len(copies):
+                copies[i + 3].start()
+
     for k in range(2):
         arrived(2 * k)
         gate = jnp.dot(xs_ref[...], gate_ref[k], preferred_element_type=F32)
         arrived(2 * k + 1)
         up = jnp.dot(xs_ref[...], up_ref[k], preferred_element_type=F32)
         act_ref[k] = (gate / (1.0 + jnp.exp(-gate)) * up).astype(BF16)
-    arrived(4)
-    arrived(5)
-    for d in (2, 1, 3, 0):
+    for copy in copies[4:]:
+        copy.wait()
+
+
+def down_kernel(ids, act_ref, down_ref, *outs):
+    rows, share = outs[0].shape
+    half = rows // 2
+    for d, places in ((2, (0, 1)), (1, (2, 0)), (3, (1, 2)), (0, (3, 3))):
         column = pl.ds(pl.multiple_of(ids[4 + d] * share, share), share)
         total = jnp.dot(act_ref[0], down_ref[0, :, column], preferred_element_type=F32)
         total = total + jnp.dot(act_ref[1], down_ref[1, :, column], preferred_element_type=F32)
         total = total.astype(BF16)
         for part in range(2):
             at_row = slice(part * half, (part + 1) * half)
-            outs[pieces_to_outs[d][part]][at_row, :] = total[at_row, :]
-
-
-def ffn(ids, gain, weights, pieces, targets):
-    rows, share = pieces[0].shape
-    depth, width = weights[0].shape[-2:]
-    outs = (jax.ShapeDtypeStruct((rows, share), BF16),) * 4
-    scratch = [pltpu.VMEM((rows, depth), BF16), pltpu.VMEM((2, rows, width), BF16)]
+            outs[places[part]][at_row, :] = total[at_row, :]
+
+
+def expert_call(kernel, inputs, weights, outs, scratch):
     spec = VMEM_SPEC
-    if len(weights) == 6:
-        shapes = (weights[0].shape, weights[1].shape, weights[4].shape)
-        outs += tuple(jax.ShapeDtypeStruct((2,) + shape, BF16) for shape in shapes)
-        scratch.append(pltpu.SemaphoreType.DMA((6,)))
+    if weights[0].ndim == 2:
+        kinds = (weights[0], weights[1], weights[4])
+        outs += tuple(jax.ShapeDtypeStruct((2,) + w.shape, BF16) for w in kinds)
+        scratch = scratch + [pltpu.SemaphoreType.DMA((len(weights),))]
         spec = HBM_SPEC
     return pl.pallas_call(
-        functools.partial(ffn_kernel, len(pieces), targets),
+        kernel,
         out_shape=outs,
-        in_specs=[SMEM_SPEC] + [VMEM_SPEC] * (1 + len(pieces)) + [spec] * len(weights),
+        in_specs=[SMEM_SPEC] + [VMEM_SPEC] * (len(inputs) - 1) + [spec] * len(weights),
         out_specs=(VMEM_SPEC,) * len(outs),
         scratch_shapes=scratch,
         compiler_params=pltpu.CompilerParams(vmem_limit_bytes=16 * MIB),
-    )(ids, gain, *pieces, *weights)
+    )(*inputs, *weights)
+
+
+def hidden(ids, gain, weights, pieces):
+    rows = pieces[0].shape[0]
+    depth, width = weights[0].shape[-2:]
+    return expert_call(
+        functools.partial(hidden_kernel, len(pieces)),
+        (ids, gain, *pieces),
+        weights,
+        (jax.ShapeDtypeStruct((2, rows, width), BF16),),
+        [pltpu.VMEM((rows, depth), BF16)],
+    )
+
+
+def down(ids, active, weights):
+    share = weights[0].shape[-1] // NZ
+    outs = (jax.ShapeDtypeStruct((active.shape[1], share), BF16),) * 4
+    return expert_call(down_kernel, (ids, active), weights, outs, [])
 
 
 def in_vmem(value):
@@ -204,13 +224,6 @@
 
 def in_hbm(value):
     return pltpu.with_memory_space_constraint(value, pltpu.HBM)
-
-
-def gather_direct(own):
-    below = in_vmem(send_z(own, 1))
-    above = in_vmem(send_z(own, -1))
-    far = in_vmem(send_z(own, 2))
-    return [own, below, above, far]
 
 
 def split_kernel(below_ref, above_ref, low_ref, high_ref):
@@ -255,18 +268,6 @@
         out_specs=(VMEM_SPEC,) * len(heights),
         compiler_params=pltpu.CompilerParams(vmem_limit_bytes=16 * MIB),
     )(*args)
-
-
-def sum_kernel(*refs):
-    total = refs[0][...].astype(F32)
-    for ref in refs[1:-1]:
-        total = total + ref[...].astype(F32)
-    refs[-1][...] = total.astype(BF16)
-
-
-def scatter_direct(near, above, far, rest):
-    moved = [in_vmem(send_z(v, d)) for v, d in ((near, 1), (above, -1), (far, 2))]
-    return local_call(sum_kernel, (in_hbm(rest), *moved), (rest.shape[0],))[0]
 
 
 def scatter_ring(up, down, relay, rest):
@@ -438,16 +439,16 @@
 
     gain_rows = gain_moe.reshape(NZ, 2 * share)
     ids = lax.rem(z + jnp.array([0, 3, 1, 2, 0, 1, 2, 3], jnp.int32), NZ)
-    direct_outs = ((3, 3), (0, 0), (2, 2), (1, 1))
-    ring_outs = ((3, 3), (2, 0), (0, 1), (1, 2))
     a_own = dispatch(picks[0])
     a_pieces = gather_ring(a_own)
     b_own = dispatch(picks[1])
-    b_pieces = gather_direct(b_own)
-    *a_out, g_held, u_held, d_held = ffn(ids, gain_rows, weights, a_pieces, direct_outs)
-    held = [in_vmem(w) for w in (g_held, u_held, d_held)]
-    b_out = ffn(ids, gain_rows, held, b_pieces, ring_outs)
-    a_final = scatter_direct(*a_out)
+    b_pieces = gather_ring(b_own)
+    a_act, *held = hidden(ids, gain_rows, weights, a_pieces)
+    held = [in_vmem(w) for w in held]
+    a_out = down(ids, a_act, held[2:])
+    (b_act,) = hidden(ids, gain_rows, held[:2], b_pieces)
+    b_out = down(ids, b_act, held[2:])
+    a_final = scatter_ring(*a_out)
     b_final = scatter_ring(*b_out)
     a_back = exchange(a_final)
     b_back = exchange(b_final)

time: 194 us -> 210 us (1.082)
  the two profiles are of different devices: /device:TPU:33 before, /device:TPU:1 now
where the time goes in v1:
time: 210 us; the launch traced here: 209 us
  starting transfers between devices  67.9 us (32%)
  waiting for transfers between devices  54.3 us (26%)
  Pallas kernels  41.2 us (20%)
  blocking collectives  13.6 us (6%)
  other arithmetic  12.2 us (6%)
  matrix products  11.1 us (5%)
  local copies, waits for them, and re-layouts  7.67 us (4%)
    ppermute x19, waiting for transfers between devices, send_z(): return lax.ppermute(value, 'tensor', z_perm(step))  27.9 us
    ppermute x19, starting transfers between devices, send_z(): return lax.ppermute(value, 'tensor', z_perm(step))  23.7 us
    pallas_call x4, Pallas kernels, expert_call(): pl.pallas_call(kernel, out_shape=outs, in_specs=[SMEM_SPEC] + [VMEM_SPEC]...  22.5 us
    all_to_all x3, starting transfers between devices, exchange(): lax.all_to_all(flat.reshape(seq_count, slots, 2 * share), 'seq', 0, 0, ti...  21.5 us
    ppermute x6, starting transfers between devices, send_core(): return lax.ppermute(value, 'tensor', core_perm())  14.9 us
    all_to_all x1, blocking collectives, exchange(): lax.all_to_all(flat.reshape(seq_count, slots, 2 * share), 'seq', 0, 0, ti...  13.6 us
    all_to_all x1, waiting for transfers between devices, local(): lax.all_to_all(jnp.broadcast_to(kv_own[None], (seq_count,) + kv_own.shape...  10.8 us
    pallas_call x6, Pallas kernels, local_call(): pl.pallas_call(kernel, out_shape=tuple((jax.ShapeDtypeStruct((height, sha...  7.62 us
  transfers between devices with their start and end apart: 31, of which 13 were waited for; matrix products, arithmetic and copies ran while one was open for 9% of the time, Pallas kernels for 20%

profile of v1, /device:TPU:1, one launch (start us, length us, event | category | flops | bytes accessed | tf_op | source)
XLA Modules:
  0.0 209.1 jit_solution(7623700750208757550)
XLA Ops:
  1.9 1.5 fusion
  3.4 1.7 fusion.11
  5.6 1.1 broadcast_in_dim.109
  6.6 7.6 %all-to-all-start = ((bf16[16,128,256]{2,1,0:T(8,128)(2,1)}), bf16[16,128,256]{2,1,0:T(8,128)(2,1)S(1)}, u32[]{:S(2)}, u32[]{:S(2)}) async-start(bf16[16,128,256]{2,1,0:T(8,128)(2,1)} %broadcast_in_dim.109), calls=%async_computation | async-start | bytes 2097152 | tf_op jit(solution)/shard_map/all_to_all | solution.py:366
  16.0 2.9 %fusion.13 = f32[128,512]{1,0:T(8,128)S(1)} fusion(bf16[4096,512]{1,0:T(8,128)(2,1)} %param.19, bf16[128,4096]{1,0:T(8,128)(2,1)S(1)} %copy-done.13, f32[4096]{0:T(1024)S(1)} %copy-done.29, f32[128]{0:T(128)S(1)} %add_rsqrt_fusion), kind=kOutput, calls=%fused_computation.26 | convolution fusion | flops 538968064 | bytes 5521920 | tf_op jit(solution)/shard_map/dot_general | solution.py:357
  19.4 10.8 %all-to-all-done = bf16[16,128,256]{2,1,0:T(8,128)(2,1)S(1)} async-done(((bf16[16,128,256]{2,1,0:T(8,128)(2,1)}), bf16[16,128,256]{2,1,0:T(8,128)(2,1)S(1)}, u32[]{:S(2)}, u32[]{:S(2)}) %all-to-all-start) | async-done | bytes 1048608 | tf_op jit(solution)/shard_map/all_to_all | solution.py:366
  30.3 6.2 %shard_map.149 = (f32[4,128,512]{2,1,0:T(8,128)S(1)}, bf16[4,128,512]{2,1,0:T(8,128)(2,1)S(1)}) custom-call(s32[8]{0:T(128)S(1)} %pad_add_fusion.ids, s32[1]{0:T(128)} %bitcast.first_ref, bf16[512,128]{1,0:T(8,128)(2,1)S(1)} %maximum_maximum_fusion.q_ref, s32[128,1]{1,0:T(8,128)S(1)} %copy.19.start_ref, bf16[2048,256]{1,0:T(8,128)(2,1)S(1)} %bitcast.71, ...), custom_call_target="tpu_custom_call" | custom-call | tf_op jit(solution)/shard_map/pallas_call | solution.py:98
  36.5 2.7 %collective-permute-start = (bf16[4,128,512]{2,1,0:T(8,128)(2,1)S(1)}, bf16[4,128,512]{2,1,0:T(8,128)(2,1)}, u32[]{:S(2)}, u32[]{:S(2)}) collective-permute-start(bf16[4,128,512]{2,1,0:T(8,128)(2,1)S(1)} %get-tuple-element.25), channel_id=1, source_target_pairs={{0,1},{1,0},{2,3},{3,2},{4,5},{5,4},{6,7},{7,6},{8,9},{9,8},{10,11... | collective-permute-start | bytes 1572872 | tf_op jit(solution)/shard_map/ppermute | solution.py:43
  39.2 1.7 collective-permute-done
  40.9 1.2 fusion.22
  42.0 1.7 collective-permute-start.1
  44.4 2.2 %collective-permute-start.2 = (bf16[128,512]{1,0:T(8,128)(2,1)S(1)}, bf16[128,512]{1,0:T(8,128)(2,1)S(1)}, u32[]{:S(2)}, u32[]{:S(2)}) collective-permute-start(bf16[128,512]{1,0:T(8,128)(2,1)S(1)} %get-tuple-element.50), channel_id=1, source_target_pairs={{0,6},{1,7},{2,0},{3,1},{4,2},{5,3},{6,4},{7,5},{8,14},{9,15},{10,... | collective-permute-start | bytes 393224 | tf_op jit(solution)/shard_map/ppermute | solution.py:39
  46.5 2.8 %collective-permute-done.1 = bf16[128,512]{1,0:T(8,128)(2,1)S(1)} collective-permute-done((bf16[128,512]{1,0:T(8,128)(2,1)S(1)}, bf16[128,512]{1,0:T(8,128)(2,1)S(1)}, u32[]{:S(2)}, u32[]{:S(2)}) %collective-permute-start.1) | collective-permute-done | bytes 131104 | tf_op jit(solution)/shard_map/ppermute | solution.py:39
  50.4 4.3 %collective-permute-done.3 = bf16[128,512]{1,0:T(8,128)(2,1)S(1)} collective-permute-done((bf16[128,512]{1,0:T(8,128)(2,1)S(1)}, bf16[128,512]{1,0:T(8,128)(2,1)S(1)}, u32[]{:S(2)}, u32[]{:S(2)}) %collective-permute-start.3) | collective-permute-done | bytes 131104 | tf_op jit(solution)/shard_map/ppermute | solution.py:39
  55.8 2.2 %collective-permute-start.4 = (bf16[128,512]{1,0:T(8,128)(2,1)S(1)}, bf16[128,512]{1,0:T(8,128)(2,1)S(1)}, u32[]{:S(2)}, u32[]{:S(2)}) collective-permute-start(bf16[128,512]{1,0:T(8,128)(2,1)S(1)} %fusion.18), channel_id=1, source_target_pairs={{0,1},{1,0},{2,3},{3,2},{4,5},{5,4},{6,7},{7,6},{8,9},{9,8},{10,11... | collective-permute-start | bytes 393224 | tf_op jit(solution)/shard_map/ppermute | solution.py:43
  59.3 13.6 %all_to_all.25 = bf16[16,16,1024]{2,1,0:T(8,128)(2,1)S(1)} all-to-all(bf16[16,16,1024]{2,1,0:T(8,128)(2,1)S(1)} %bitcast.81), channel_id=1, replica_groups=mesh['seq'=16,'tensor'=8] {'seq'}, dimensions={0} | all-to-all | bytes 1048576 | tf_op jit(solution)/shard_map/all_to_all | solution.py:414
  72.9 2.7 %collective-permute-start.8 = (bf16[256,1024]{1,0:T(8,128)(2,1)S(1)}, bf16[256,1024]{1,0:T(8,128)(2,1)S(1)}, u32[]{:S(2)}, u32[]{:S(2)}) collective-permute-start(bf16[256,1024]{1,0:T(8,128)(2,1)S(1)} %bitcast.77), channel_id=1, source_target_pairs={{0,6},{1,7},{2,0},{3,1},{4,2},{5,3},{6,4},{7,5},{8,14},{9,15},{10,... | collective-permute-start | bytes 1572872 | tf_op jit(solution)/shard_map/ppermute | solution.py:39
  75.5 1.1 convolution_convert_fusion
  76.6 3.6 %all-to-all-start.3 = ((bf16[16,16,1024]{2,1,0:T(8,128)(2,1)}), bf16[16,16,1024]{2,1,0:T(8,128)(2,1)S(1)}, u32[]{:S(2)}, u32[]{:S(2)}) async-start(bf16[16,16,1024]{2,1,0:T(8,128)(2,1)} %bitcast.80), calls=%async_computation.3 | async-start | bytes 1048576 | tf_op jit(solution)/shard_map/all_to_all | solution.py:414
  80.2 5.8 %collective-permute-done.7.below_ref.refs_1_ = bf16[256,1024]{1,0:T(8,128)(2,1)S(1)} collective-permute-done((bf16[256,1024]{1,0:T(8,128)(2,1)S(1)}, bf16[256,1024]{1,0:T(8,128)(2,1)S(1)}, u32[]{:S(2)}, u32[]{:S(2)}) %collective-permute-start.7) | collective-permute-done | bytes 524320 | tf_op jit(solution)/shard_map/ppermute | solution.py:39
  86.9 2.4 %collective-permute-start.10 = (bf16[128,1024]{1,0:T(8,128)(2,1)}, bf16[128,1024]{1,0:T(8,128)(2,1)S(1)}, u32[]{:S(2)}, u32[]{:S(2)}) collective-permute-start(bf16[128,1024]{1,0:T(8,128)(2,1)} %get-tuple-element.27), channel_id=1, source_target_pairs={{0,6},{1,7},{2,0},{3,1},{4,2},{5,3},{6,4},{7,5},{8,14},{9,15},{10,... | collective-permute-start | bytes 786440 | tf_op jit(solution)/shard_map/ppermute | solution.py:39
  89.8 3.2 %collective-permute-done.10.refs_4_ = bf16[128,1024]{1,0:T(8,128)(2,1)S(1)} collective-permute-done((bf16[128,1024]{1,0:T(8,128)(2,1)}, bf16[128,1024]{1,0:T(8,128)(2,1)S(1)}, u32[]{:S(2)}, u32[]{:S(2)}) %collective-permute-start.10) | collective-permute-done | bytes 262176 | tf_op jit(solution)/shard_map/ppermute | solution.py:39
  93.0 3.1 %collective-permute-done.9.refs_3_ = bf16[128,1024]{1,0:T(8,128)(2,1)} collective-permute-done((bf16[128,1024]{1,0:T(8,128)(2,1)}, bf16[128,1024]{1,0:T(8,128)(2,1)}, u32[]{:S(2)}, u32[]{:S(2)}) %collective-permute-start.9) | collective-permute-done | bytes 262176 | tf_op jit(solution)/shard_map/ppermute | solution.py:39
  98.4 1.1 fusion.10
  101.7 9.4 %shard_map.151 = (bf16[2,256,512]{2,1,0:T(8,128)(2,1)S(1)}, bf16[2,4096,512]{2,1,0:T(8,128)(2,1)S(1)}, bf16[2,4096,512]{2,1,0:T(8,128)(2,1)S(1)}, bf16[2,512,4096]{2,1,0:T(8,128)(2,1)S(1)}) custom-call(s32[8]{0:T(128)S(1)} %compare_select_fusion.1.ids, f32[4,1024]{1,0:T(4,128)S(1)} %reshape.172.gain_ref, bf16[256,1024]{1,0:T(8,128)(2,1)S(1)} %bitcast.78, ...), custom_call_target="tpu_custom_call" | custom-call | tf_op jit(solution)/shard_map/pallas_call | solution.py:193
  111.2 2.9 %shard_map.152 = (bf16[256,1024]{1,0:T(8,128)(2,1)S(1)}, bf16[256,1024]{1,0:T(8,128)(2,1)S(1)}, bf16[256,1024]{1,0:T(8,128)(2,1)S(1)}, bf16[256,1024]{1,0:T(8,128)(2,1)S(1)}) custom-call(s32[8]{0:T(128)S(1)} %compare_select_fusion.1.ids, bf16[2,256,512]{2,1,0:T(8,128)(2,1)S(1)} %get-tuple-element.28.act_ref, bf16[2,512,4096]{2,1,0:T(8,128)(2,1)S(1)} %get-tuple-element.29.down_ref), custom_call_target="tpu_custom_call" | custom-call | tf_op jit(solution)/shard_map/pallas_call | solution.py:193
  114.8 1.3 collective-permute-start.14
  116.1 1.4 collective-permute-start.15
  117.5 1.3 fusion.9
  119.1 2.6 %collective-permute-start.21 = (bf16[128,1024]{1,0:T(8,128)(2,1)S(1)}, bf16[128,1024]{1,0:T(8,128)(2,1)S(1)}, u32[]{:S(2)}, u32[]{:S(2)}) collective-permute-start(bf16[128,1024]{1,0:T(8,128)(2,1)S(1)} %get-tuple-element.37), channel_id=1, source_target_pairs={{0,6},{1,7},{2,0},{3,1},{4,2},{5,3},{6,4},{7,5},{8,14},{9,15},{10,... | collective-permute-start | bytes 786440 | tf_op jit(solution)/shard_map/ppermute | solution.py:39
  122.7 6.1 %collective-permute-done.20.refs_3_ = bf16[128,1024]{1,0:T(8,128)(2,1)S(1)} collective-permute-done((bf16[128,1024]{1,0:T(8,128)(2,1)S(1)}, bf16[128,1024]{1,0:T(8,128)(2,1)S(1)}, u32[]{:S(2)}, u32[]{:S(2)}) %collective-permute-start.20) | collective-permute-done | bytes 262176 | tf_op jit(solution)/shard_map/ppermute | solution.py:39
  128.8 6.7 %shard_map.156.act_ref = bf16[2,256,512]{2,1,0:T(8,128)(2,1)S(1)} custom-call(s32[8]{0:T(128)S(1)} %compare_select_fusion.1.ids, f32[4,1024]{1,0:T(4,128)S(1)} %reshape.172.gain_ref, bf16[256,1024]{1,0:T(8,128)(2,1)S(1)} %bitcast.75, bf16[256,1024]{1,0:T(8,128)(2,1)S(1)} %collective-permute-done.18.below_ref.refs_1_, ...), custom_call_target="tpu_custom_call" | custom-call | tf_op jit(solution)/shard_map/pallas_call | solution.py:193
  135.5 3.4 %shard_map.157 = (bf16[256,1024]{1,0:T(8,128)(2,1)}, bf16[256,1024]{1,0:T(8,128)(2,1)S(1)}, bf16[256,1024]{1,0:T(8,128)(2,1)S(1)}, bf16[256,1024]{1,0:T(8,128)(2,1)S(1)}) custom-call(s32[8]{0:T(128)S(1)} %compare_select_fusion.1.ids, bf16[2,256,512]{2,1,0:T(8,128)(2,1)S(1)} %shard_map.156.act_ref, bf16[2,512,4096]{2,1,0:T(8,128)(2,1)S(1)} %get-tuple-element.29.down_ref), custom_call_target="tpu_custom_call" | custom-call | tf_op jit(solution)/shard_map/pallas_call | solution.py:193
  139.0 2.7 %collective-permute-start.23 = (bf16[256,1024]{1,0:T(8,128)(2,1)S(1)}, bf16[256,1024]{1,0:T(8,128)(2,1)S(1)}, u32[]{:S(2)}, u32[]{:S(2)}) collective-permute-start(bf16[256,1024]{1,0:T(8,128)(2,1)S(1)} %get-tuple-element.42), channel_id=1, source_target_pairs={{0,6},{1,7},{2,0},{3,1},{4,2},{5,3},{6,4},{7,5},{8,14},{9,15},{10,... | collective-permute-start | bytes 1572872 | tf_op jit(solution)/shard_map/ppermute | solution.py:39
  141.6 1.2 shard_map.153
  142.9 2.7 %collective-permute-start.17 = (bf16[128,1024]{1,0:T(8,128)(2,1)S(1)}, bf16[128,1024]{1,0:T(8,128)(2,1)S(1)}, u32[]{:S(2)}, u32[]{:S(2)}) collective-permute-start(bf16[128,1024]{1,0:T(8,128)(2,1)S(1)} %get-tuple-element.35), channel_id=1, source_target_pairs={{0,6},{1,7},{2,0},{3,1},{4,2},{5,3},{6,4},{7,5},{8,14},{9,15},{10,... | collective-permute-start | bytes 786440 | tf_op jit(solution)/shard_map/ppermute | solution.py:39
  146.3 6.5 %collective-permute-done.6 = f32[128,16]{0,1:T(8,128)S(1)} collective-permute-done((f32[128,16]{0,1:T(8,128)S(1)}, f32[128,16]{0,1:T(8,128)S(1)}, u32[]{:S(2)}, u32[]{:S(2)}) %collective-permute-start.6) | collective-permute-done | bytes 8224 | tf_op jit(solution)/shard_map/ppermute | solution.py:432
  153.6 2.2 %shard_map.154 = bf16[256,1024]{1,0:T(8,128)(2,1)} custom-call(bf16[256,1024]{1,0:T(8,128)(2,1)} %copy-done.6, bf16[256,1024]{1,0:T(8,128)(2,1)S(1)} %collective-permute-done.14.below_ref, bf16[256,1024]{1,0:T(8,128)(2,1)S(1)} %collective-permute-done.15.above_ref, bf16[128,1024]{1,0:T(8,128)(2,1)} %copy-done.16, bf16[128,1024]{1,0:T(8,128)(2,1)} %copy-done.17), custom_call_target="tpu_custom_call" | custom-call | tf_op jit(solution)/shard_map/pallas_call | solution.py:264
  155.8 11.0 %all-to-all-start.2 = ((bf16[16,16,1024]{2,1,0:T(8,128)(2,1)}), bf16[16,16,1024]{2,1,0:T(8,128)(2,1)S(1)}, u32[]{:S(2)}, u32[]{:S(2)}) async-start(bf16[16,16,1024]{2,1,0:T(8,128)(2,1)} %bitcast.17), calls=%async_computation.2 | async-start | bytes 1048576 | tf_op jit(solution)/shard_map/all_to_all | solution.py:414
  166.8 1.2 shard_map.158
  168.4 2.3 %collective-permute-start.25 = (bf16[128,1024]{1,0:T(8,128)(2,1)S(1)}, bf16[128,1024]{1,0:T(8,128)(2,1)}, u32[]{:S(2)}, u32[]{:S(2)}) collective-permute-start(bf16[128,1024]{1,0:T(8,128)(2,1)S(1)} %get-tuple-element.45), channel_id=1, source_target_pairs={{0,6},{1,7},{2,0},{3,1},{4,2},{5,3},{6,4},{7,5},{8,14},{9,15},{10,... | collective-permute-start | bytes 786440 | tf_op jit(solution)/shard_map/ppermute | solution.py:39
  172.0 2.5 %collective-permute-done.24.low_ref = bf16[128,1024]{1,0:T(8,128)(2,1)S(1)} collective-permute-done((bf16[128,1024]{1,0:T(8,128)(2,1)S(1)}, bf16[128,1024]{1,0:T(8,128)(2,1)S(1)}, u32[]{:S(2)}, u32[]{:S(2)}) %collective-permute-start.24) | collective-permute-done | bytes 262176 | tf_op jit(solution)/shard_map/ppermute | solution.py:39
  175.2 2.2 %shard_map.159 = bf16[256,1024]{1,0:T(8,128)(2,1)} custom-call(bf16[256,1024]{1,0:T(8,128)(2,1)} %copy-done.7, bf16[256,1024]{1,0:T(8,128)(2,1)S(1)} %collective-permute-done.22.below_ref, bf16[256,1024]{1,0:T(8,128)(2,1)S(1)} %collective-permute-done.23.above_ref, bf16[128,1024]{1,0:T(8,128)(2,1)} %copy-done.18, ...), custom_call_target="tpu_custom_call" | custom-call | tf_op jit(solution)/shard_map/pallas_call | solution.py:264
  177.4 6.9 %all-to-all-start.4 = ((bf16[16,16,1024]{2,1,0:T(8,128)(2,1)}), bf16[16,16,1024]{2,1,0:T(8,128)(2,1)S(1)}, u32[]{:S(2)}, u32[]{:S(2)}) async-start(bf16[16,16,1024]{2,1,0:T(8,128)(2,1)} %bitcast.22), calls=%async_computation.4 | async-start | bytes 1048576 | tf_op jit(solution)/shard_map/all_to_all | solution.py:414
  185.1 1.8 convolution_bitcast_fusion.2
  186.8 6.5 %all-to-all-done.4 = bf16[16,16,1024]{2,1,0:T(8,128)(2,1)S(1)} async-done(((bf16[16,16,1024]{2,1,0:T(8,128)(2,1)}), bf16[16,16,1024]{2,1,0:T(8,128)(2,1)S(1)}, u32[]{:S(2)}, u32[]{:S(2)}) %all-to-all-start.4) | async-done | bytes 524320 | tf_op jit(solution)/shard_map/all_to_all | solution.py:414
  194.9 8.5 %collective-permute-start.26 = (bf16[128,512]{1,0:T(8,128)(2,1)S(1)}, bf16[128,512]{1,0:T(8,128)(2,1)S(1)}, u32[]{:S(2)}, u32[]{:S(2)}) collective-permute-start(bf16[128,512]{1,0:T(8,128)(2,1)S(1)} %select_convert_fusion), channel_id=1, source_target_pairs={{0,1},{1,0},{2,3},{3,2},{4,5},{5,4},{6,7},{7,6},{8,9},{9,8},{10,11... | collective-permute-start | bytes 393224 | tf_op jit(solution)/shard_map/ppermute | solution.py:43
  203.5 4.9 %shard_map.160 = bf16[2048,256]{1,0:T(8,128)(2,1)} custom-call(s32[1,2048]{1,0:T(1,128)S(1)} %bitcast.79, bf16[2048,256]{1,0:T(8,128)(2,1)S(1)} %bitcast.72), custom_call_target="tpu_custom_call" | custom-call | tf_op jit(solution)/shard_map/pallas_call | solution.py:297
  (153 shorter events, 22.8 us)
Async XLA Ops:
  5.1 10.9 %copy-start.13 = (bf16[128,4096]{1,0:T(8,128)(2,1)S(1)}, bf16[128,4096]{1,0:T(8,128)(2,1)}, u32[]{:S(2)}) copy-start(bf16[128,4096]{1,0:T(8,128)(2,1)} %param.14) | copy-start | bytes 3145732
  5.1 10.9 %copy-start.29 = (f32[4096]{0:T(1024)S(1)}, f32[4096]{0:T(1024)}, u32[]{:S(2)}) copy-start(f32[4096]{0:T(1024)} %param.18) | copy-start | bytes 49156
  6.6 23.6 %all-to-all-start = ((bf16[16,128,256]{2,1,0:T(8,128)(2,1)}), bf16[16,128,256]{2,1,0:T(8,128)(2,1)S(1)}, u32[]{:S(2)}, u32[]{:S(2)}) async-start(bf16[16,128,256]{2,1,0:T(8,128)(2,1)} %broadcast_in_dim.109), calls=%async_computation | async-start | bytes 2097152 | tf_op jit(solution)/shard_map/all_to_all | solution.py:366
  14.2 85.3 %collective-permute-start.11 = (bf16[4096,512]{1,0:T(8,128)(2,1)}, bf16[4096,512]{1,0:T(8,128)(2,1)}, u32[]{:S(2)}, u32[]{:S(2)}) collective-permute-start(bf16[4096,512]{1,0:T(8,128)(2,1)} %refs_5_.1), channel_id=1, source_target_pairs={{0,1},{1,0},{2,3},{3,2},{4,5},{5,4},{6,7},{7,6},{8,9},{9,8},{10,11... | collective-permute-start | bytes 12582920 | tf_op jit(solution)/shard_map/ppermute | solution.py:43
  15.3 84.3 %collective-permute-start.12 = (bf16[4096,512]{1,0:T(8,128)(2,1)}, bf16[4096,512]{1,0:T(8,128)(2,1)}, u32[]{:S(2)}, u32[]{:S(2)}) collective-permute-start(bf16[4096,512]{1,0:T(8,128)(2,1)} %refs_6_.1), channel_id=1, source_target_pairs={{0,1},{1,0},{2,3},{3,2},{4,5},{5,4},{6,7},{7,6},{8,9},{9,8},{10,11... | collective-permute-start | bytes 12582920 | tf_op jit(solution)/shard_map/ppermute | solution.py:43
  15.4 84.2 %collective-permute-start.13 = (bf16[512,4096]{1,0:T(8,128)(2,1)}, bf16[512,4096]{1,0:T(8,128)(2,1)}, u32[]{:S(2)}, u32[]{:S(2)}) collective-permute-start(bf16[512,4096]{1,0:T(8,128)(2,1)} %refs_9_.1), channel_id=1, source_target_pairs={{0,1},{1,0},{2,3},{3,2},{4,5},{5,4},{6,7},{7,6},{8,9},{9,8},{10,11... | collective-permute-start | bytes 12582920 | tf_op jit(solution)/shard_map/ppermute | solution.py:43
  30.3 20.1 %copy-start.22 = (s32[128,2]{0,1:T(2,128)S(1)}, s32[128,2]{0,1:T(2,128)}, u32[]{:S(2)}) copy-start(s32[128,2]{0,1:T(2,128)} %param.16) | copy-start | bytes 3076
  36.5 4.3 %collective-permute-start = (bf16[4,128,512]{2,1,0:T(8,128)(2,1)S(1)}, bf16[4,128,512]{2,1,0:T(8,128)(2,1)}, u32[]{:S(2)}, u32[]{:S(2)}) collective-permute-start(bf16[4,128,512]{2,1,0:T(8,128)(2,1)S(1)} %get-tuple-element.25), channel_id=1, source_target_pairs={{0,1},{1,0},{2,3},{3,2},{4,5},{5,4},{6,7},{7,6},{8,9},{9,8},{10,11... | collective-permute-start | bytes 1572872 | tf_op jit(solution)/shard_map/ppermute | solution.py:43
  42.0 7.3 %collective-permute-start.1 = (bf16[128,512]{1,0:T(8,128)(2,1)S(1)}, bf16[128,512]{1,0:T(8,128)(2,1)S(1)}, u32[]{:S(2)}, u32[]{:S(2)}) collective-permute-start(bf16[128,512]{1,0:T(8,128)(2,1)S(1)} %get-tuple-element.48), channel_id=1, source_target_pairs={{0,2},{1,3},{2,4},{3,5},{4,6},{5,7},{6,0},{7,1},{8,10},{9,11},{10,... | collective-permute-start | bytes 393224 | tf_op jit(solution)/shard_map/ppermute | solution.py:39
  44.4 6.0 %collective-permute-start.2 = (bf16[128,512]{1,0:T(8,128)(2,1)S(1)}, bf16[128,512]{1,0:T(8,128)(2,1)S(1)}, u32[]{:S(2)}, u32[]{:S(2)}) collective-permute-start(bf16[128,512]{1,0:T(8,128)(2,1)S(1)} %get-tuple-element.50), channel_id=1, source_target_pairs={{0,6},{1,7},{2,0},{3,1},{4,2},{5,3},{6,4},{7,5},{8,14},{9,15},{10,... | collective-permute-start | bytes 393224 | tf_op jit(solution)/shard_map/ppermute | solution.py:39
  49.4 5.3 %collective-permute-start.3 = (bf16[128,512]{1,0:T(8,128)(2,1)S(1)}, bf16[128,512]{1,0:T(8,128)(2,1)S(1)}, u32[]{:S(2)}, u32[]{:S(2)}) collective-permute-start(bf16[128,512]{1,0:T(8,128)(2,1)S(1)} %get-tuple-element.49), channel_id=1, source_target_pairs={{0,4},{1,5},{2,6},{3,7},{4,0},{5,1},{6,2},{7,3},{8,12},{9,13},{10,... | collective-permute-start | bytes 393224 | tf_op jit(solution)/shard_map/ppermute | solution.py:39
  55.8 3.2 %collective-permute-start.4 = (bf16[128,512]{1,0:T(8,128)(2,1)S(1)}, bf16[128,512]{1,0:T(8,128)(2,1)S(1)}, u32[]{:S(2)}, u32[]{:S(2)}) collective-permute-start(bf16[128,512]{1,0:T(8,128)(2,1)S(1)} %fusion.18), channel_id=1, source_target_pairs={{0,1},{1,0},{2,3},{3,2},{4,5},{5,4},{6,7},{7,6},{8,9},{9,8},{10,11... | collective-permute-start | bytes 393224 | tf_op jit(solution)/shard_map/ppermute | solution.py:43
  58.2 18.4 %copy-start.14 = (s32[8,2,128]{2,1,0:T(2,128)}, s32[8,2,128]{2,1,0:T(2,128)S(1)}, u32[]{:S(2)}) copy-start(s32[8,2,128]{2,1,0:T(2,128)S(1)} %broadcast_in_dim.111) | copy-start | bytes 24580
  58.9 17.7 %copy-start.19 = (bf16[128,512]{1,0:T(8,128)(2,1)}, bf16[128,512]{1,0:T(8,128)(2,1)S(1)}, u32[]{:S(2)}) copy-start(bf16[128,512]{1,0:T(8,128)(2,1)S(1)} %collective-permute-done.4) | copy-start | bytes 393220
  59.2 30.1 %copy-start.30 = (s32[15]{0:T(128)S(1)}, s32[15]{0:T(128)}, u32[]{:S(2)}) copy-start(s32[15]{0:T(128)} %param.17) | copy-start | bytes 184
  72.9 13.2 %collective-permute-start.7 = (bf16[256,1024]{1,0:T(8,128)(2,1)S(1)}, bf16[256,1024]{1,0:T(8,128)(2,1)S(1)}, u32[]{:S(2)}, u32[]{:S(2)}) collective-permute-start(bf16[256,1024]{1,0:T(8,128)(2,1)S(1)} %bitcast.76), channel_id=1, source_target_pairs={{0,2},{1,3},{2,4},{3,5},{4,6},{5,7},{6,0},{7,1},{8,10},{9,11},{10,... | collective-permute-start | bytes 1572872 | tf_op jit(solution)/shard_map/ppermute | solution.py:39
  72.9 13.2 %collective-permute-start.8 = (bf16[256,1024]{1,0:T(8,128)(2,1)S(1)}, bf16[256,1024]{1,0:T(8,128)(2,1)S(1)}, u32[]{:S(2)}, u32[]{:S(2)}) collective-permute-start(bf16[256,1024]{1,0:T(8,128)(2,1)S(1)} %bitcast.77), channel_id=1, source_target_pairs={{0,6},{1,7},{2,0},{3,1},{4,2},{5,3},{6,4},{7,5},{8,14},{9,15},{10,... | collective-permute-start | bytes 1572872 | tf_op jit(solution)/shard_map/ppermute | solution.py:39
  76.6 13.2 %all-to-all-start.3 = ((bf16[16,16,1024]{2,1,0:T(8,128)(2,1)}), bf16[16,16,1024]{2,1,0:T(8,128)(2,1)S(1)}, u32[]{:S(2)}, u32[]{:S(2)}) async-start(bf16[16,16,1024]{2,1,0:T(8,128)(2,1)} %bitcast.80), calls=%async_computation.3 | async-start | bytes 1048576 | tf_op jit(solution)/shard_map/all_to_all | solution.py:414
  86.9 6.0 %collective-permute-start.10 = (bf16[128,1024]{1,0:T(8,128)(2,1)}, bf16[128,1024]{1,0:T(8,128)(2,1)S(1)}, u32[]{:S(2)}, u32[]{:S(2)}) collective-permute-start(bf16[128,1024]{1,0:T(8,128)(2,1)} %get-tuple-element.27), channel_id=1, source_target_pairs={{0,6},{1,7},{2,0},{3,1},{4,2},{5,3},{6,4},{7,5},{8,14},{9,15},{10,... | collective-permute-start | bytes 786440 | tf_op jit(solution)/shard_map/ppermute | solution.py:39
  89.3 6.7 %collective-permute-start.9 = (bf16[128,1024]{1,0:T(8,128)(2,1)}, bf16[128,1024]{1,0:T(8,128)(2,1)}, u32[]{:S(2)}, u32[]{:S(2)}) collective-permute-start(bf16[128,1024]{1,0:T(8,128)(2,1)} %get-tuple-element.26), channel_id=1, source_target_pairs={{0,2},{1,3},{2,4},{3,5},{4,6},{5,7},{6,0},{7,1},{8,10},{9,11},{10,... | collective-permute-start | bytes 786440 | tf_op jit(solution)/shard_map/ppermute | solution.py:39
  93.0 25.9 %collective-permute-start.18 = (bf16[256,1024]{1,0:T(8,128)(2,1)S(1)}, bf16[256,1024]{1,0:T(8,128)(2,1)S(1)}, u32[]{:S(2)}, u32[]{:S(2)}) collective-permute-start(bf16[256,1024]{1,0:T(8,128)(2,1)S(1)} %bitcast.73), channel_id=1, source_target_pairs={{0,2},{1,3},{2,4},{3,5},{4,6},{5,7},{6,0},{7,1},{8,10},{9,11},{10,... | collective-permute-start | bytes 1572872 | tf_op jit(solution)/shard_map/ppermute | solution.py:39
  96.1 22.8 %collective-permute-start.19 = (bf16[256,1024]{1,0:T(8,128)(2,1)S(1)}, bf16[256,1024]{1,0:T(8,128)(2,1)S(1)}, u32[]{:S(2)}, u32[]{:S(2)}) collective-permute-start(bf16[256,1024]{1,0:T(8,128)(2,1)S(1)} %bitcast.74), channel_id=1, source_target_pairs={{0,6},{1,7},{2,0},{3,1},{4,2},{5,3},{6,4},{7,5},{8,14},{9,15},{10,... | collective-permute-start | bytes 1572872 | tf_op jit(solution)/shard_map/ppermute | solution.py:39
  114.8 20.7 %copy-start.6 = (bf16[256,1024]{1,0:T(8,128)(2,1)}, bf16[256,1024]{1,0:T(8,128)(2,1)S(1)}, u32[]{:S(2)}) copy-start(bf16[256,1024]{1,0:T(8,128)(2,1)S(1)} %get-tuple-element.30.rest_ref) | copy-start | bytes 1572868
  114.8 26.8 %collective-permute-start.14 = (bf16[256,1024]{1,0:T(8,128)(2,1)S(1)}, bf16[256,1024]{1,0:T(8,128)(2,1)S(1)}, u32[]{:S(2)}, u32[]{:S(2)}) collective-permute-start(bf16[256,1024]{1,0:T(8,128)(2,1)S(1)} %get-tuple-element.31), channel_id=1, source_target_pairs={{0,2},{1,3},{2,4},{3,5},{4,6},{5,7},{6,0},{7,1},{8,10},{9,11},{10,... | collective-permute-start | bytes 1572872 | tf_op jit(solution)/shard_map/ppermute | solution.py:39
  116.1 25.5 %collective-permute-start.15 = (bf16[256,1024]{1,0:T(8,128)(2,1)S(1)}, bf16[256,1024]{1,0:T(8,128)(2,1)S(1)}, u32[]{:S(2)}, u32[]{:S(2)}) collective-permute-start(bf16[256,1024]{1,0:T(8,128)(2,1)S(1)} %get-tuple-element.32), channel_id=1, source_target_pairs={{0,6},{1,7},{2,0},{3,1},{4,2},{5,3},{6,4},{7,5},{8,14},{9,15},{10,... | collective-permute-start | bytes 1572872 | tf_op jit(solution)/shard_map/ppermute | solution.py:39
  118.9 9.9 %collective-permute-start.20 = (bf16[128,1024]{1,0:T(8,128)(2,1)S(1)}, bf16[128,1024]{1,0:T(8,128)(2,1)S(1)}, u32[]{:S(2)}, u32[]{:S(2)}) collective-permute-start(bf16[128,1024]{1,0:T(8,128)(2,1)S(1)} %get-tuple-element.36), channel_id=1, source_target_pairs={{0,2},{1,3},{2,4},{3,5},{4,6},{5,7},{6,0},{7,1},{8,10},{9,11},{10,... | collective-permute-start | bytes 786440 | tf_op jit(solution)/shard_map/ppermute | solution.py:39
  119.1 9.7 %collective-permute-start.21 = (bf16[128,1024]{1,0:T(8,128)(2,1)S(1)}, bf16[128,1024]{1,0:T(8,128)(2,1)S(1)}, u32[]{:S(2)}, u32[]{:S(2)}) collective-permute-start(bf16[128,1024]{1,0:T(8,128)(2,1)S(1)} %get-tuple-element.37), channel_id=1, source_target_pairs={{0,6},{1,7},{2,0},{3,1},{4,2},{5,3},{6,4},{7,5},{8,14},{9,15},{10,... | collective-permute-start | bytes 786440 | tf_op jit(solution)/shard_map/ppermute | solution.py:39
  121.7 23.9 %collective-permute-start.5 = (f32[128,16]{0,1:T(8,128)S(1)}, f32[128,16]{0,1:T(8,128)S(1)}, u32[]{:S(2)}, u32[]{:S(2)}) collective-permute-start(f32[128,16]{0,1:T(8,128)S(1)} %maximum_maximum_fusion.1), channel_id=1, source_target_pairs={{0,2},{1,3},{2,0},{3,1},{4,6},{5,7},{6,4},{7,5},{8,10},{9,11},{10,... | collective-permute-start | bytes 24584 | tf_op jit(solution)/shard_map/ppermute | solution.py:431
  139.0 16.8 %copy-start.7 = (bf16[256,1024]{1,0:T(8,128)(2,1)}, bf16[256,1024]{1,0:T(8,128)(2,1)S(1)}, u32[]{:S(2)}) copy-start(bf16[256,1024]{1,0:T(8,128)(2,1)S(1)} %get-tuple-element.40.rest_ref) | copy-start | bytes 1572868
  139.0 16.8 %copy-start.9 = (bf16[256,1024]{1,0:T(8,128)(2,1)}, bf16[256,1024]{1,0:T(8,128)(2,1)S(1)}, u32[]{:S(2)}) copy-start(bf16[256,1024]{1,0:T(8,128)(2,1)S(1)} %get-tuple-element.43.relay_ref) | copy-start | bytes 1572868
  139.0 27.8 %collective-permute-start.22 = (bf16[256,1024]{1,0:T(8,128)(2,1)}, bf16[256,1024]{1,0:T(8,128)(2,1)S(1)}, u32[]{:S(2)}, u32[]{:S(2)}) collective-permute-start(bf16[256,1024]{1,0:T(8,128)(2,1)} %get-tuple-element.41), channel_id=1, source_target_pairs={{0,2},{1,3},{2,4},{3,5},{4,6},{5,7},{6,0},{7,1},{8,10},{9,11},{10,... | collective-permute-start | bytes 1572872 | tf_op jit(solution)/shard_map/ppermute | solution.py:39
  139.0 27.8 %collective-permute-start.23 = (bf16[256,1024]{1,0:T(8,128)(2,1)S(1)}, bf16[256,1024]{1,0:T(8,128)(2,1)S(1)}, u32[]{:S(2)}, u32[]{:S(2)}) collective-permute-start(bf16[256,1024]{1,0:T(8,128)(2,1)S(1)} %get-tuple-element.42), channel_id=1, source_target_pairs={{0,6},{1,7},{2,0},{3,1},{4,2},{5,3},{6,4},{7,5},{8,14},{9,15},{10,... | collective-permute-start | bytes 1572872 | tf_op jit(solution)/shard_map/ppermute | solution.py:39
  142.8 10.0 %collective-permute-start.16 = (bf16[128,1024]{1,0:T(8,128)(2,1)S(1)}, bf16[128,1024]{1,0:T(8,128)(2,1)S(1)}, u32[]{:S(2)}, u32[]{:S(2)}) collective-permute-start(bf16[128,1024]{1,0:T(8,128)(2,1)S(1)} %get-tuple-element.34), channel_id=1, source_target_pairs={{0,2},{1,3},{2,4},{3,5},{4,6},{5,7},{6,0},{7,1},{8,10},{9,11},{10,... | collective-permute-start | bytes 786440 | tf_op jit(solution)/shard_map/ppermute | solution.py:39
  142.9 9.9 %collective-permute-start.17 = (bf16[128,1024]{1,0:T(8,128)(2,1)S(1)}, bf16[128,1024]{1,0:T(8,128)(2,1)S(1)}, u32[]{:S(2)}, u32[]{:S(2)}) collective-permute-start(bf16[128,1024]{1,0:T(8,128)(2,1)S(1)} %get-tuple-element.35), channel_id=1, source_target_pairs={{0,6},{1,7},{2,0},{3,1},{4,2},{5,3},{6,4},{7,5},{8,14},{9,15},{10,... | collective-permute-start | bytes 786440 | tf_op jit(solution)/shard_map/ppermute | solution.py:39
  145.7 7.1 %collective-permute-start.6 = (f32[128,16]{0,1:T(8,128)S(1)}, f32[128,16]{0,1:T(8,128)S(1)}, u32[]{:S(2)}, u32[]{:S(2)}) collective-permute-start(f32[128,16]{0,1:T(8,128)S(1)} %fusion.104), channel_id=1, source_target_pairs={{0,4},{1,5},{2,6},{3,7},{4,0},{5,1},{6,2},{7,3},{8,12},{9,13},{10,... | collective-permute-start | bytes 24584 | tf_op jit(solution)/shard_map/ppermute | solution.py:432
  155.8 21.6 %all-to-all-start.2 = ((bf16[16,16,1024]{2,1,0:T(8,128)(2,1)}), bf16[16,16,1024]{2,1,0:T(8,128)(2,1)S(1)}, u32[]{:S(2)}, u32[]{:S(2)}) async-start(bf16[16,16,1024]{2,1,0:T(8,128)(2,1)} %bitcast.17), calls=%async_computation.2 | async-start | bytes 1048576 | tf_op jit(solution)/shard_map/all_to_all | solution.py:414
  168.0 17.1 %copy-start.15 = (s32[8,2,128]{2,1,0:T(2,128)S(1)}, s32[8,2,128]{2,1,0:T(2,128)}, u32[]{:S(2)}) copy-start(s32[8,2,128]{2,1,0:T(2,128)} %copy-done.14) | copy-start | bytes 24580
  168.0 6.5 %collective-permute-start.24 = (bf16[128,1024]{1,0:T(8,128)(2,1)S(1)}, bf16[128,1024]{1,0:T(8,128)(2,1)S(1)}, u32[]{:S(2)}, u32[]{:S(2)}) collective-permute-start(bf16[128,1024]{1,0:T(8,128)(2,1)S(1)} %get-tuple-element.44), channel_id=1, source_target_pairs={{0,2},{1,3},{2,4},{3,5},{4,6},{5,7},{6,0},{7,1},{8,10},{9,11},{10,... | collective-permute-start | bytes 786440 | tf_op jit(solution)/shard_map/ppermute | solution.py:39
  168.4 6.1 %collective-permute-start.25 = (bf16[128,1024]{1,0:T(8,128)(2,1)S(1)}, bf16[128,1024]{1,0:T(8,128)(2,1)}, u32[]{:S(2)}, u32[]{:S(2)}) collective-permute-start(bf16[128,1024]{1,0:T(8,128)(2,1)S(1)} %get-tuple-element.45), channel_id=1, source_target_pairs={{0,6},{1,7},{2,0},{3,1},{4,2},{5,3},{6,4},{7,5},{8,14},{9,15},{10,... | collective-permute-start | bytes 786440 | tf_op jit(solution)/shard_map/ppermute | solution.py:39
  174.5 9.8 %copy-start.27 = (f32[128]{0:T(128)S(1)}, f32[128]{0:T(128)}, u32[]{:S(2)}) copy-start(f32[128]{0:T(128)} %reduce_max.9) | copy-start | bytes 1540
  175.2 18.1 %copy-start.24 = (s32[16]{0:T(128)S(1)}, s32[16]{0:T(128)}, u32[]{:S(2)}) copy-start(s32[16]{0:T(128)} %copy-done.23) | copy-start | bytes 196
  177.4 7.7 %copy-start.10 = (bf16[16,16,1024]{2,1,0:T(8,128)(2,1)}, bf16[16,16,1024]{2,1,0:T(8,128)(2,1)S(1)}, u32[]{:S(2)}) copy-start(bf16[16,16,1024]{2,1,0:T(8,128)(2,1)S(1)} %all-to-all-done.2) | copy-start | bytes 1572868
  177.4 15.9 %all-to-all-start.4 = ((bf16[16,16,1024]{2,1,0:T(8,128)(2,1)}), bf16[16,16,1024]{2,1,0:T(8,128)(2,1)S(1)}, u32[]{:S(2)}, u32[]{:S(2)}) async-start(bf16[16,16,1024]{2,1,0:T(8,128)(2,1)} %bitcast.22), calls=%async_computation.4 | async-start | bytes 1048576 | tf_op jit(solution)/shard_map/all_to_all | solution.py:414
  184.3 9.7 %copy-start.26 = (s32[16]{0:T(128)S(1)}, s32[16]{0:T(128)}, u32[]{:S(2)}) copy-start(s32[16]{0:T(128)} %copy-done.25) | copy-start | bytes 196
  193.6 9.7 %copy-start.28 = (pred[2048]{0:T(1024)(128)(4,1)S(1)}, pred[2048]{0:T(1024)(128)(4,1)}, u32[]{:S(2)}) copy-start(pred[2048]{0:T(1024)(128)(4,1)} %get-tuple-element.47) | copy-start | bytes 6148
  193.6 9.7 %copy-start.31 = (f32[16]{0:T(128)S(1)}, f32[16]{0:T(128)}, u32[]{:S(2)}) copy-start(f32[16]{0:T(128)} %convolution_bitcast_fusion.4) | copy-start | bytes 196
  194.5 14.6 %copy-start.1 = (bf16[4096,256]{1,0:T(8,128)(2,1)S(1)}, bf16[4096,256]{1,0:T(8,128)(2,1)}, u32[]{:S(2)}) copy-start(bf16[4096,256]{1,0:T(8,128)(2,1)} %param.20) | copy-start | bytes 6291460
  194.9 13.5 %collective-permute-start.26 = (bf16[128,512]{1,0:T(8,128)(2,1)S(1)}, bf16[128,512]{1,0:T(8,128)(2,1)S(1)}, u32[]{:S(2)}, u32[]{:S(2)}) collective-permute-start(bf16[128,512]{1,0:T(8,128)(2,1)S(1)} %select_convert_fusion), channel_id=1, source_target_pairs={{0,1},{1,0},{2,3},{3,2},{4,5},{5,4},{6,7},{7,6},{8,9},{9,8},{10,11... | collective-permute-start | bytes 393224 | tf_op jit(solution)/shard_map/ppermute | solution.py:43
  (16 other events, 45.0 us)

commit v2 on v1

--- a/solution.py
+++ b/solution.py
@@ -232,14 +232,14 @@
     high_ref[...] = above_ref[half:, :]
 
 
-def gather_ring(own):
+def gather_ring(own, place):
     half = own.shape[0] // 2
-    below = in_vmem(send_z(own, 1))
-    above = in_vmem(send_z(own, -1))
+    below = send_z(own, 1)
+    above = send_z(own, -1)
     low, high = local_call(split_kernel, (below, above), (half, half))
     far_a = in_vmem(send_z(low, 1))
     far_b = in_vmem(send_z(high, -1))
-    return [own, below, above, far_a, far_b]
+    return [own, place(below), place(above), far_a, far_b]
 
 
 def relay_kernel(relay_ref, below_ref, above_ref, low_ref, high_ref):
@@ -270,18 +270,18 @@
     )(*args)
 
 
-def scatter_ring(up, down, relay, rest):
+def scatter_ring(up, down, relay, rest, place):
     rows = up.shape[0]
     half = rows // 2
     from_below = in_vmem(send_z(up, 1))
     from_above = in_vmem(send_z(down, -1))
     low, high = local_call(
-        relay_kernel, (in_hbm(relay), from_below, from_above), (half, half)
-    )
-    low = in_hbm(send_z(in_hbm(low), 1))
-    high = in_hbm(send_z(in_hbm(high), -1))
+        relay_kernel, (place(relay), from_below, from_above), (half, half)
+    )
+    low = place(send_z(place(low), 1))
+    high = place(send_z(place(high), -1))
     moved = (from_below, from_above, low, high)
-    return local_call(end_kernel, (in_hbm(rest), *moved), (rows,))[0]
+    return local_call(end_kernel, (place(rest), *moved), (rows,))[0]
 
 
 def cache_kernel(slot_ref, kv_ref, out_ref):
@@ -440,16 +440,16 @@
     gain_rows = gain_moe.reshape(NZ, 2 * share)
     ids = lax.rem(z + jnp.array([0, 3, 1, 2, 0, 1, 2, 3], jnp.int32), NZ)
     a_own = dispatch(picks[0])
-    a_pieces = gather_ring(a_own)
+    a_pieces = gather_ring(a_own, in_hbm)
     b_own = dispatch(picks[1])
-    b_pieces = gather_ring(b_own)
+    b_pieces = gather_ring(b_own, in_vmem)
     a_act, *held = hidden(ids, gain_rows, weights, a_pieces)
     held = [in_vmem(w) for w in held]
     a_out = down(ids, a_act, held[2:])
     (b_act,) = hidden(ids, gain_rows, held[:2], b_pieces)
     b_out = down(ids, b_act, held[2:])
-    a_final = scatter_ring(*a_out)
-    b_final = scatter_ring(*b_out)
+    a_final = scatter_ring(*a_out, in_vmem)
+    b_final = scatter_ring(*b_out, in_hbm)
     a_back = exchange(a_final)
     b_back = exchange(b_final)
 
@@ -462,7 +462,7 @@
             low, back, preferred_element_type=F32
         )
 
-    mixture = combine(picks[0], a_back) + combine(picks[1], b_back)
+    mixture = lax.optimization_barrier(combine(picks[0], a_back)) + combine(picks[1], b_back)
     left, right = mixture[:, :share], mixture[:, share:]
     theirs = send_core(jnp.where(c == 0, right, left).astype(BF16))
     mine = jnp.where(c == 0, left, right)

time: 210 us -> 195 us (0.929)
  the two profiles are of different devices: /device:TPU:1 before, /device:TPU:33 now
where the time goes in v2:
time: 195 us; the launch traced here: 193 us
  starting transfers between devices  66.7 us (34%)
  waiting for transfers between devices  47.9 us (25%)
  Pallas kernels  38.7 us (20%)
  blocking collectives  13.6 us (7%)
  matrix products  12.4 us (6%)
  other arithmetic  8.61 us (4%)
  local copies, waits for them, and re-layouts  3.49 us (2%)
    ppermute x19, waiting for transfers between devices, send_z(): return lax.ppermute(value, 'tensor', z_perm(step))  24.1 us
    pallas_call x4, Pallas kernels, expert_call(): pl.pallas_call(kernel, out_shape=outs, in_specs=[SMEM_SPEC] + [VMEM_SPEC]...  22.2 us
    ppermute x19, starting transfers between devices, send_z(): return lax.ppermute(value, 'tensor', z_perm(step))  22.2 us
    ppermute x6, starting transfers between devices, send_core(): return lax.ppermute(value, 'tensor', core_perm())  19.4 us
    all_to_all x3, starting transfers between devices, exchange(): lax.all_to_all(flat.reshape(seq_count, slots, 2 * share), 'seq', 0, 0, ti...  15.5 us
    all_to_all x1, blocking collectives, exchange(): lax.all_to_all(flat.reshape(seq_count, slots, 2 * share), 'seq', 0, 0, ti...  13.6 us
    all_to_all x1, waiting for transfers between devices, local(): lax.all_to_all(jnp.broadcast_to(kv_own[None], (seq_count,) + kv_own.shape...  10.8 us
    all_to_all x1, starting transfers between devices, local(): lax.all_to_all(jnp.broadcast_to(kv_own[None], (seq_count,) + kv_own.shape...  6.75 us
  transfers between devices with their start and end apart: 31, of which 15 were waited for; matrix products, arithmetic and copies ran while one was open for 8% of the time, Pallas kernels for 20%

profile of v2, /device:TPU:33, one launch (start us, length us, event | category | flops | bytes accessed | tf_op | source)
XLA Modules:
  0.0 192.5 jit_solution(13962264471506240916)
XLA Ops:
  1.9 1.5 fusion
  3.4 1.7 fusion.10
  6.6 6.8 %all-to-all-start = ((bf16[16,128,256]{2,1,0:T(8,128)(2,1)}), bf16[16,128,256]{2,1,0:T(8,128)(2,1)S(1)}, u32[]{:S(2)}, u32[]{:S(2)}) async-start(bf16[16,128,256]{2,1,0:T(8,128)(2,1)} %broadcast_in_dim.109), calls=%async_computation | async-start | bytes 2097152 | tf_op jit(solution)/shard_map/all_to_all | solution.py:366
  15.2 2.9 %fusion.12 = f32[128,512]{1,0:T(8,128)S(1)} fusion(bf16[4096,512]{1,0:T(8,128)(2,1)} %param.19, bf16[128,4096]{1,0:T(8,128)(2,1)S(1)} %copy-done.7, f32[4096]{0:T(1024)S(1)} %copy-done.15, f32[128]{0:T(128)S(1)} %add_rsqrt_fusion), kind=kOutput, calls=%fused_computation.25 | convolution fusion | flops 538968064 | bytes 5521920 | tf_op jit(solution)/shard_map/dot_general | solution.py:357
  18.6 10.8 %all-to-all-done = bf16[16,128,256]{2,1,0:T(8,128)(2,1)S(1)} async-done(((bf16[16,128,256]{2,1,0:T(8,128)(2,1)}), bf16[16,128,256]{2,1,0:T(8,128)(2,1)S(1)}, u32[]{:S(2)}, u32[]{:S(2)}) %all-to-all-start) | async-done | bytes 1048608 | tf_op jit(solution)/shard_map/all_to_all | solution.py:366
  29.5 6.3 %shard_map.149 = (f32[4,128,512]{2,1,0:T(8,128)S(1)}, bf16[4,128,512]{2,1,0:T(8,128)(2,1)S(1)}) custom-call(s32[8]{0:T(128)S(1)} %pad_add_fusion.ids, s32[1]{0:T(128)} %bitcast.first_ref, bf16[512,128]{1,0:T(8,128)(2,1)S(1)} %maximum_maximum_fusion.q_ref, s32[128,1]{1,0:T(8,128)S(1)} %copy.19.start_ref, bf16[2048,256]{1,0:T(8,128)(2,1)S(1)} %bitcast.69, ...), custom_call_target="tpu_custom_call" | custom-call | tf_op jit(solution)/shard_map/pallas_call | solution.py:98
  35.7 2.7 %collective-permute-start = (bf16[4,128,512]{2,1,0:T(8,128)(2,1)S(1)}, bf16[4,128,512]{2,1,0:T(8,128)(2,1)}, u32[]{:S(2)}, u32[]{:S(2)}) collective-permute-start(bf16[4,128,512]{2,1,0:T(8,128)(2,1)S(1)} %get-tuple-element.25), channel_id=1, source_target_pairs={{0,1},{1,0},{2,3},{3,2},{4,5},{5,4},{6,7},{7,6},{8,9},{9,8},{10,11... | collective-permute-start | bytes 1572872 | tf_op jit(solution)/shard_map/ppermute | solution.py:43
  38.4 1.7 collective-permute-done
  40.1 1.2 fusion.21
  41.2 1.7 collective-permute-start.1
  43.1 2.8 %collective-permute-done.1 = bf16[128,512]{1,0:T(8,128)(2,1)S(1)} collective-permute-done((bf16[128,512]{1,0:T(8,128)(2,1)S(1)}, bf16[128,512]{1,0:T(8,128)(2,1)S(1)}, u32[]{:S(2)}, u32[]{:S(2)}) %collective-permute-start.1) | collective-permute-done | bytes 131104 | tf_op jit(solution)/shard_map/ppermute | solution.py:39
  46.0 2.7 %collective-permute-start.3 = (bf16[128,512]{1,0:T(8,128)(2,1)S(1)}, bf16[128,512]{1,0:T(8,128)(2,1)S(1)}, u32[]{:S(2)}, u32[]{:S(2)}) collective-permute-start(bf16[128,512]{1,0:T(8,128)(2,1)S(1)} %get-tuple-element.49), channel_id=1, source_target_pairs={{0,4},{1,5},{2,6},{3,7},{4,0},{5,1},{6,2},{7,3},{8,12},{9,13},{10,... | collective-permute-start | bytes 393224 | tf_op jit(solution)/shard_map/ppermute | solution.py:39
  48.7 2.6 %collective-permute-done.3 = bf16[128,512]{1,0:T(8,128)(2,1)S(1)} collective-permute-done((bf16[128,512]{1,0:T(8,128)(2,1)S(1)}, bf16[128,512]{1,0:T(8,128)(2,1)S(1)}, u32[]{:S(2)}, u32[]{:S(2)}) %collective-permute-start.3) | collective-permute-done | bytes 131104 | tf_op jit(solution)/shard_map/ppermute | solution.py:39
  52.4 2.5 %collective-permute-start.4 = (bf16[128,512]{1,0:T(8,128)(2,1)S(1)}, bf16[128,512]{1,0:T(8,128)(2,1)S(1)}, u32[]{:S(2)}, u32[]{:S(2)}) collective-permute-start(bf16[128,512]{1,0:T(8,128)(2,1)S(1)} %fusion.17), channel_id=1, source_target_pairs={{0,1},{1,0},{2,3},{3,2},{4,5},{5,4},{6,7},{7,6},{8,9},{9,8},{10,11... | collective-permute-start | bytes 393224 | tf_op jit(solution)/shard_map/ppermute | solution.py:43
  56.2 13.6 %all_to_all.25 = bf16[16,16,1024]{2,1,0:T(8,128)(2,1)S(1)} all-to-all(bf16[16,16,1024]{2,1,0:T(8,128)(2,1)S(1)} %bitcast.79), channel_id=1, replica_groups=mesh['seq'=16,'tensor'=8] {'seq'}, dimensions={0} | all-to-all | bytes 1048576 | tf_op jit(solution)/shard_map/all_to_all | solution.py:414
  69.8 1.6 collective-permute-start.7
  71.9 1.1 convolution_convert_fusion
  73.0 3.6 %all-to-all-start.3 = ((bf16[16,16,1024]{2,1,0:T(8,128)(2,1)}), bf16[16,16,1024]{2,1,0:T(8,128)(2,1)S(1)}, u32[]{:S(2)}, u32[]{:S(2)}) async-start(bf16[16,16,1024]{2,1,0:T(8,128)(2,1)} %bitcast.78), calls=%async_computation.3 | async-start | bytes 1048576 | tf_op jit(solution)/shard_map/all_to_all | solution.py:414
  76.7 6.0 %collective-permute-done.7.below_ref.refs_1_ = bf16[256,1024]{1,0:T(8,128)(2,1)S(1)} collective-permute-done((bf16[256,1024]{1,0:T(8,128)(2,1)S(1)}, bf16[256,1024]{1,0:T(8,128)(2,1)S(1)}, u32[]{:S(2)}, u32[]{:S(2)}) %collective-permute-start.7) | collective-permute-done | bytes 524320 | tf_op jit(solution)/shard_map/ppermute | solution.py:39
  84.0 2.0 %collective-permute-start.10 = (bf16[128,1024]{1,0:T(8,128)(2,1)}, bf16[128,1024]{1,0:T(8,128)(2,1)S(1)}, u32[]{:S(2)}, u32[]{:S(2)}) collective-permute-start(bf16[128,1024]{1,0:T(8,128)(2,1)} %get-tuple-element.27), channel_id=1, source_target_pairs={{0,6},{1,7},{2,0},{3,1},{4,2},{5,3},{6,4},{7,5},{8,14},{9,15},{10,... | collective-permute-start | bytes 786440 | tf_op jit(solution)/shard_map/ppermute | solution.py:39
  86.3 1.3 fusion.9
  87.5 2.1 %collective-permute-done.10.refs_4_ = bf16[128,1024]{1,0:T(8,128)(2,1)S(1)} collective-permute-done((bf16[128,1024]{1,0:T(8,128)(2,1)}, bf16[128,1024]{1,0:T(8,128)(2,1)S(1)}, u32[]{:S(2)}, u32[]{:S(2)}) %collective-permute-start.10) | collective-permute-done | bytes 262176 | tf_op jit(solution)/shard_map/ppermute | solution.py:39
  89.7 2.5 %collective-permute-start.18 = (bf16[256,1024]{1,0:T(8,128)(2,1)S(1)}, bf16[256,1024]{1,0:T(8,128)(2,1)S(1)}, u32[]{:S(2)}, u32[]{:S(2)}) collective-permute-start(bf16[256,1024]{1,0:T(8,128)(2,1)S(1)} %bitcast.71), channel_id=1, source_target_pairs={{0,2},{1,3},{2,4},{3,5},{4,6},{5,7},{6,0},{7,1},{8,10},{9,11},{10,... | collective-permute-start | bytes 1572872 | tf_op jit(solution)/shard_map/ppermute | solution.py:39
  92.6 2.5 %collective-permute-start.19 = (bf16[256,1024]{1,0:T(8,128)(2,1)S(1)}, bf16[256,1024]{1,0:T(8,128)(2,1)S(1)}, u32[]{:S(2)}, u32[]{:S(2)}) collective-permute-start(bf16[256,1024]{1,0:T(8,128)(2,1)S(1)} %bitcast.72), channel_id=1, source_target_pairs={{0,6},{1,7},{2,0},{3,1},{4,2},{5,3},{6,4},{7,5},{8,14},{9,15},{10,... | collective-permute-start | bytes 1572872 | tf_op jit(solution)/shard_map/ppermute | solution.py:39
  95.1 1.6 fusion.8
  96.8 9.8 %shard_map.151 = (bf16[2,256,512]{2,1,0:T(8,128)(2,1)S(1)}, bf16[2,4096,512]{2,1,0:T(8,128)(2,1)S(1)}, bf16[2,4096,512]{2,1,0:T(8,128)(2,1)S(1)}, bf16[2,512,4096]{2,1,0:T(8,128)(2,1)S(1)}) custom-call(s32[8]{0:T(128)S(1)} %compare_select_fusion.1.ids, f32[4,1024]{1,0:T(4,128)S(1)} %reshape.172.gain_ref, bf16[256,1024]{1,0:T(8,128)(2,1)S(1)} %bitcast.76, ...), custom_call_target="tpu_custom_call" | custom-call | tf_op jit(solution)/shard_map/pallas_call | solution.py:193
  106.6 2.9 %shard_map.152 = (bf16[256,1024]{1,0:T(8,128)(2,1)S(1)}, bf16[256,1024]{1,0:T(8,128)(2,1)S(1)}, bf16[256,1024]{1,0:T(8,128)(2,1)S(1)}, bf16[256,1024]{1,0:T(8,128)(2,1)S(1)}) custom-call(s32[8]{0:T(128)S(1)} %compare_select_fusion.1.ids, bf16[2,256,512]{2,1,0:T(8,128)(2,1)S(1)} %get-tuple-element.28.act_ref, bf16[2,512,4096]{2,1,0:T(8,128)(2,1)S(1)} %get-tuple-element.29.down_ref), custom_call_target="tpu_custom_call" | custom-call | tf_op jit(solution)/shard_map/pallas_call | solution.py:193
  109.6 1.5 collective-permute-start.15
  111.1 1.2 collective-permute-start.5
  112.6 1.5 collective-permute-start.21
  114.0 3.6 %collective-permute-done.5 = f32[128,16]{0,1:T(8,128)S(1)} collective-permute-done((f32[128,16]{0,1:T(8,128)S(1)}, f32[128,16]{0,1:T(8,128)S(1)}, u32[]{:S(2)}, u32[]{:S(2)}) %collective-permute-start.5) | collective-permute-done | bytes 8224 | tf_op jit(solution)/shard_map/ppermute | solution.py:431
  117.7 1.6 collective-permute-start.6
  119.5 1.1 collective-permute-start.16
  121.1 1.7 collective-permute-done.6
  122.8 6.7 %shard_map.156.act_ref = bf16[2,256,512]{2,1,0:T(8,128)(2,1)S(1)} custom-call(s32[8]{0:T(128)S(1)} %compare_select_fusion.1.ids, f32[4,1024]{1,0:T(4,128)S(1)} %reshape.172.gain_ref, bf16[256,1024]{1,0:T(8,128)(2,1)S(1)} %bitcast.73, bf16[256,1024]{1,0:T(8,128)(2,1)S(1)} %collective-permute-done.18.below_ref.refs_1_, ...), custom_call_target="tpu_custom_call" | custom-call | tf_op jit(solution)/shard_map/pallas_call | solution.py:193
  129.5 2.9 %shard_map.157 = (bf16[256,1024]{1,0:T(8,128)(2,1)S(1)}, bf16[256,1024]{1,0:T(8,128)(2,1)S(1)}, bf16[256,1024]{1,0:T(8,128)(2,1)S(1)}, bf16[256,1024]{1,0:T(8,128)(2,1)S(1)}) custom-call(s32[8]{0:T(128)S(1)} %compare_select_fusion.1.ids, bf16[2,256,512]{2,1,0:T(8,128)(2,1)S(1)} %shard_map.156.act_ref, bf16[2,512,4096]{2,1,0:T(8,128)(2,1)S(1)} %get-tuple-element.29.down_ref), custom_call_target="tpu_custom_call" | custom-call | tf_op jit(solution)/shard_map/pallas_call | solution.py:193
  133.6 2.2 %collective-permute-start.23 = (bf16[256,1024]{1,0:T(8,128)(2,1)S(1)}, bf16[256,1024]{1,0:T(8,128)(2,1)S(1)}, u32[]{:S(2)}, u32[]{:S(2)}) collective-permute-start(bf16[256,1024]{1,0:T(8,128)(2,1)S(1)} %get-tuple-element.42), channel_id=1, source_target_pairs={{0,6},{1,7},{2,0},{3,1},{4,2},{5,3},{6,4},{7,5},{8,14},{9,15},{10,... | collective-permute-start | bytes 1572872 | tf_op jit(solution)/shard_map/ppermute | solution.py:39
  136.8 6.7 %all-to-all-start.2 = ((bf16[16,16,1024]{2,1,0:T(8,128)(2,1)}), bf16[16,16,1024]{2,1,0:T(8,128)(2,1)}, u32[]{:S(2)}, u32[]{:S(2)}) async-start(bf16[16,16,1024]{2,1,0:T(8,128)(2,1)} %bitcast.17), calls=%async_computation.2 | async-start | bytes 1048576 | tf_op jit(solution)/shard_map/all_to_all | solution.py:414
  144.6 1.2 shard_map.158
  147.3 6.8 %collective-permute-done.24.low_ref = bf16[128,1024]{1,0:T(8,128)(2,1)S(1)} collective-permute-done((bf16[128,1024]{1,0:T(8,128)(2,1)S(1)}, bf16[128,1024]{1,0:T(8,128)(2,1)S(1)}, u32[]{:S(2)}, u32[]{:S(2)}) %collective-permute-start.24) | collective-permute-done | bytes 262176 | tf_op jit(solution)/shard_map/ppermute | solution.py:39
  154.1 1.8 collective-permute-done.25.high_ref
  156.6 2.2 %shard_map.159 = bf16[256,1024]{1,0:T(8,128)(2,1)} custom-call(bf16[256,1024]{1,0:T(8,128)(2,1)} %copy-done.4, bf16[256,1024]{1,0:T(8,128)(2,1)S(1)} %collective-permute-done.22.below_ref, bf16[256,1024]{1,0:T(8,128)(2,1)S(1)} %collective-permute-done.23.above_ref, bf16[128,1024]{1,0:T(8,128)(2,1)} %copy-done.10, bf16[128,1024]{1,0:T(8,128)(2,1)} %copy-done.11), custom_call_target="tpu_custom_call" | custom-call | tf_op jit(solution)/shard_map/pallas_call | solution.py:264
  158.7 5.2 %all-to-all-start.4 = ((bf16[16,16,1024]{2,1,0:T(8,128)(2,1)}), bf16[16,16,1024]{2,1,0:T(8,128)(2,1)S(1)}, u32[]{:S(2)}, u32[]{:S(2)}) async-start(bf16[16,16,1024]{2,1,0:T(8,128)(2,1)} %bitcast.22), calls=%async_computation.4 | async-start | bytes 1048576 | tf_op jit(solution)/shard_map/all_to_all | solution.py:414
  164.0 1.4 convolution_bitcast_fusion.2
  165.3 2.2 %fusion.3 = f32[128,1024]{1,0:T(8,128)} fusion(f32[128,1024]{1,0:T(8,128)S(1)} %convolution_bitcast_fusion.2, bf16[16,16,1024]{2,1,0:T(8,128)(2,1)} %all-to-all-done.2, f32[128,16]{0,1:T(8,128)S(1)} %bitcast.86, s32[128,16]{0,1:T(8,128)S(1)} %bitcast.82, s32[16]{0:T(128)S(1)} %iota_add_fusion.1), kind=kOutput, calls=%fused_computation.11 | convolution fusion | flops 67305472 | bytes 1589312 | tf_op jit(solution)/shard_map/dot_general | solution.py:461
  167.5 5.4 %all-to-all-done.4 = bf16[16,16,1024]{2,1,0:T(8,128)(2,1)S(1)} async-done(((bf16[16,16,1024]{2,1,0:T(8,128)(2,1)}), bf16[16,16,1024]{2,1,0:T(8,128)(2,1)S(1)}, u32[]{:S(2)}, u32[]{:S(2)}) %all-to-all-start.4) | async-done | bytes 524320 | tf_op jit(solution)/shard_map/all_to_all | solution.py:414
  174.1 12.7 %collective-permute-start.26 = (bf16[128,512]{1,0:T(8,128)(2,1)S(1)}, bf16[128,512]{1,0:T(8,128)(2,1)S(1)}, u32[]{:S(2)}, u32[]{:S(2)}) collective-permute-start(bf16[128,512]{1,0:T(8,128)(2,1)S(1)} %select_convert_fusion), channel_id=1, source_target_pairs={{0,1},{1,0},{2,3},{3,2},{4,5},{5,4},{6,7},{7,6},{8,9},{9,8},{10,11... | collective-permute-start | bytes 393224 | tf_op jit(solution)/shard_map/ppermute | solution.py:43
  186.9 4.9 %shard_map.160 = bf16[2048,256]{1,0:T(8,128)(2,1)} custom-call(s32[1,2048]{1,0:T(1,128)S(1)} %bitcast.77, bf16[2048,256]{1,0:T(8,128)(2,1)S(1)} %bitcast.70), custom_call_target="tpu_custom_call" | custom-call | tf_op jit(solution)/shard_map/pallas_call | solution.py:297
  (125 shorter events, 18.7 us)
Async XLA Ops:
  0.6 2.8 %copy-start = (bf16[4096,256]{1,0:T(8,128)(2,1)S(1)}, bf16[4096,256]{1,0:T(8,128)(2,1)}, u32[]{:S(2)}) copy-start(bf16[4096,256]{1,0:T(8,128)(2,1)} %param.20) | copy-start | bytes 6291460
  5.1 10.0 %copy-start.7 = (bf16[128,4096]{1,0:T(8,128)(2,1)S(1)}, bf16[128,4096]{1,0:T(8,128)(2,1)}, u32[]{:S(2)}) copy-start(bf16[128,4096]{1,0:T(8,128)(2,1)} %param.14) | copy-start | bytes 3145732
  5.1 10.0 %copy-start.15 = (f32[4096]{0:T(1024)S(1)}, f32[4096]{0:T(1024)}, u32[]{:S(2)}) copy-start(f32[4096]{0:T(1024)} %param.18) | copy-start | bytes 49156
  6.6 22.8 %all-to-all-start = ((bf16[16,128,256]{2,1,0:T(8,128)(2,1)}), bf16[16,128,256]{2,1,0:T(8,128)(2,1)S(1)}, u32[]{:S(2)}, u32[]{:S(2)}) async-start(bf16[16,128,256]{2,1,0:T(8,128)(2,1)} %broadcast_in_dim.109), calls=%async_computation | async-start | bytes 2097152 | tf_op jit(solution)/shard_map/all_to_all | solution.py:366
  13.4 83.4 %collective-permute-start.11 = (bf16[4096,512]{1,0:T(8,128)(2,1)}, bf16[4096,512]{1,0:T(8,128)(2,1)}, u32[]{:S(2)}, u32[]{:S(2)}) collective-permute-start(bf16[4096,512]{1,0:T(8,128)(2,1)} %refs_5_.1), channel_id=1, source_target_pairs={{0,1},{1,0},{2,3},{3,2},{4,5},{5,4},{6,7},{7,6},{8,9},{9,8},{10,11... | collective-permute-start | bytes 12582920 | tf_op jit(solution)/shard_map/ppermute | solution.py:43
  14.4 82.3 %collective-permute-start.12 = (bf16[4096,512]{1,0:T(8,128)(2,1)}, bf16[4096,512]{1,0:T(8,128)(2,1)}, u32[]{:S(2)}, u32[]{:S(2)}) collective-permute-start(bf16[4096,512]{1,0:T(8,128)(2,1)} %refs_6_.1), channel_id=1, source_target_pairs={{0,1},{1,0},{2,3},{3,2},{4,5},{5,4},{6,7},{7,6},{8,9},{9,8},{10,11... | collective-permute-start | bytes 12582920 | tf_op jit(solution)/shard_map/ppermute | solution.py:43
  14.5 82.2 %collective-permute-start.13 = (bf16[512,4096]{1,0:T(8,128)(2,1)}, bf16[512,4096]{1,0:T(8,128)(2,1)}, u32[]{:S(2)}, u32[]{:S(2)}) collective-permute-start(bf16[512,4096]{1,0:T(8,128)(2,1)} %refs_9_.1), channel_id=1, source_target_pairs={{0,1},{1,0},{2,3},{3,2},{4,5},{5,4},{6,7},{7,6},{8,9},{9,8},{10,11... | collective-permute-start | bytes 12582920 | tf_op jit(solution)/shard_map/ppermute | solution.py:43
  29.5 19.2 %copy-start.14 = (s32[128,2]{0,1:T(2,128)S(1)}, s32[128,2]{0,1:T(2,128)}, u32[]{:S(2)}) copy-start(s32[128,2]{0,1:T(2,128)} %param.16) | copy-start | bytes 3076
  35.7 4.3 %collective-permute-start = (bf16[4,128,512]{2,1,0:T(8,128)(2,1)S(1)}, bf16[4,128,512]{2,1,0:T(8,128)(2,1)}, u32[]{:S(2)}, u32[]{:S(2)}) collective-permute-start(bf16[4,128,512]{2,1,0:T(8,128)(2,1)S(1)} %get-tuple-element.25), channel_id=1, source_target_pairs={{0,1},{1,0},{2,3},{3,2},{4,5},{5,4},{6,7},{7,6},{8,9},{9,8},{10,11... | collective-permute-start | bytes 1572872 | tf_op jit(solution)/shard_map/ppermute | solution.py:43
  41.2 4.8 %collective-permute-start.1 = (bf16[128,512]{1,0:T(8,128)(2,1)S(1)}, bf16[128,512]{1,0:T(8,128)(2,1)S(1)}, u32[]{:S(2)}, u32[]{:S(2)}) collective-permute-start(bf16[128,512]{1,0:T(8,128)(2,1)S(1)} %get-tuple-element.48), channel_id=1, source_target_pairs={{0,2},{1,3},{2,4},{3,5},{4,6},{5,7},{6,0},{7,1},{8,10},{9,11},{10,... | collective-permute-start | bytes 393224 | tf_op jit(solution)/shard_map/ppermute | solution.py:39
  43.1 5.6 %collective-permute-start.2 = (bf16[128,512]{1,0:T(8,128)(2,1)S(1)}, bf16[128,512]{1,0:T(8,128)(2,1)S(1)}, u32[]{:S(2)}, u32[]{:S(2)}) collective-permute-start(bf16[128,512]{1,0:T(8,128)(2,1)S(1)} %get-tuple-element.50), channel_id=1, source_target_pairs={{0,6},{1,7},{2,0},{3,1},{4,2},{5,3},{6,4},{7,5},{8,14},{9,15},{10,... | collective-permute-start | bytes 393224 | tf_op jit(solution)/shard_map/ppermute | solution.py:39
  46.0 5.3 %collective-permute-start.3 = (bf16[128,512]{1,0:T(8,128)(2,1)S(1)}, bf16[128,512]{1,0:T(8,128)(2,1)S(1)}, u32[]{:S(2)}, u32[]{:S(2)}) collective-permute-start(bf16[128,512]{1,0:T(8,128)(2,1)S(1)} %get-tuple-element.49), channel_id=1, source_target_pairs={{0,4},{1,5},{2,6},{3,7},{4,0},{5,1},{6,2},{7,3},{8,12},{9,13},{10,... | collective-permute-start | bytes 393224 | tf_op jit(solution)/shard_map/ppermute | solution.py:39
  52.4 19.5 %copy-start.8 = (bf16[128,512]{1,0:T(8,128)(2,1)}, bf16[128,512]{1,0:T(8,128)(2,1)S(1)}, u32[]{:S(2)}) copy-start(bf16[128,512]{1,0:T(8,128)(2,1)S(1)} %fusion.17) | copy-start | bytes 393220
  52.4 3.4 %collective-permute-start.4 = (bf16[128,512]{1,0:T(8,128)(2,1)S(1)}, bf16[128,512]{1,0:T(8,128)(2,1)S(1)}, u32[]{:S(2)}, u32[]{:S(2)}) collective-permute-start(bf16[128,512]{1,0:T(8,128)(2,1)S(1)} %fusion.17), channel_id=1, source_target_pairs={{0,1},{1,0},{2,3},{3,2},{4,5},{5,4},{6,7},{7,6},{8,9},{9,8},{10,11... | collective-permute-start | bytes 393224 | tf_op jit(solution)/shard_map/ppermute | solution.py:43
  55.8 17.2 %copy-start.12 = (bf16[128,512]{1,0:T(8,128)(2,1)}, bf16[128,512]{1,0:T(8,128)(2,1)S(1)}, u32[]{:S(2)}) copy-start(bf16[128,512]{1,0:T(8,128)(2,1)S(1)} %collective-permute-done.4) | copy-start | bytes 393220
  55.8 20.8 %copy-start.16 = (s32[15]{0:T(128)S(1)}, s32[15]{0:T(128)}, u32[]{:S(2)}) copy-start(s32[15]{0:T(128)} %param.17) | copy-start | bytes 184
  56.1 30.0 %copy-start.13 = (f32[4096]{0:T(1024)S(1)}, f32[4096]{0:T(1024)}, u32[]{:S(2)}) copy-start(f32[4096]{0:T(1024)} %param.22) | copy-start | bytes 49156
  56.2 30.1 %copy-start.17 = (s32[8]{0:T(128)S(1)}, s32[8]{0:T(128)}, u32[]{:S(2)}) copy-start(s32[8]{0:T(128)} %constant.75.clone) | copy-start | bytes 100
  69.8 12.9 %collective-permute-start.7 = (bf16[256,1024]{1,0:T(8,128)(2,1)S(1)}, bf16[256,1024]{1,0:T(8,128)(2,1)S(1)}, u32[]{:S(2)}, u32[]{:S(2)}) collective-permute-start(bf16[256,1024]{1,0:T(8,128)(2,1)S(1)} %bitcast.74), channel_id=1, source_target_pairs={{0,2},{1,3},{2,4},{3,5},{4,6},{5,7},{6,0},{7,1},{8,10},{9,11},{10,... | collective-permute-start | bytes 1572872 | tf_op jit(solution)/shard_map/ppermute | solution.py:39
  71.4 11.7 %collective-permute-start.8 = (bf16[256,1024]{1,0:T(8,128)(2,1)S(1)}, bf16[256,1024]{1,0:T(8,128)(2,1)S(1)}, u32[]{:S(2)}, u32[]{:S(2)}) collective-permute-start(bf16[256,1024]{1,0:T(8,128)(2,1)S(1)} %bitcast.75), channel_id=1, source_target_pairs={{0,6},{1,7},{2,0},{3,1},{4,2},{5,3},{6,4},{7,5},{8,14},{9,15},{10,... | collective-permute-start | bytes 1572872 | tf_op jit(solution)/shard_map/ppermute | solution.py:39
  73.0 14.5 %all-to-all-start.3 = ((bf16[16,16,1024]{2,1,0:T(8,128)(2,1)}), bf16[16,16,1024]{2,1,0:T(8,128)(2,1)S(1)}, u32[]{:S(2)}, u32[]{:S(2)}) async-start(bf16[16,16,1024]{2,1,0:T(8,128)(2,1)} %bitcast.78), calls=%async_computation.3 | async-start | bytes 1048576 | tf_op jit(solution)/shard_map/all_to_all | solution.py:414
  82.7 14.1 %copy-start.2 = (bf16[256,1024]{1,0:T(8,128)(2,1)}, bf16[256,1024]{1,0:T(8,128)(2,1)S(1)}, u32[]{:S(2)}) copy-start(bf16[256,1024]{1,0:T(8,128)(2,1)S(1)} %collective-permute-done.7.below_ref.refs_1_) | copy-start | bytes 1572868
  83.1 13.7 %copy-start.3 = (bf16[256,1024]{1,0:T(8,128)(2,1)}, bf16[256,1024]{1,0:T(8,128)(2,1)S(1)}, u32[]{:S(2)}) copy-start(bf16[256,1024]{1,0:T(8,128)(2,1)S(1)} %collective-permute-done.8.above_ref.refs_2_) | copy-start | bytes 1572868
  84.0 5.7 %collective-permute-start.10 = (bf16[128,1024]{1,0:T(8,128)(2,1)}, bf16[128,1024]{1,0:T(8,128)(2,1)S(1)}, u32[]{:S(2)}, u32[]{:S(2)}) collective-permute-start(bf16[128,1024]{1,0:T(8,128)(2,1)} %get-tuple-element.27), channel_id=1, source_target_pairs={{0,6},{1,7},{2,0},{3,1},{4,2},{5,3},{6,4},{7,5},{8,14},{9,15},{10,... | collective-permute-start | bytes 786440 | tf_op jit(solution)/shard_map/ppermute | solution.py:39
  86.0 6.6 %collective-permute-start.9 = (bf16[128,1024]{1,0:T(8,128)(2,1)}, bf16[128,1024]{1,0:T(8,128)(2,1)}, u32[]{:S(2)}, u32[]{:S(2)}) collective-permute-start(bf16[128,1024]{1,0:T(8,128)(2,1)} %get-tuple-element.26), channel_id=1, source_target_pairs={{0,2},{1,3},{2,4},{3,5},{4,6},{5,7},{6,0},{7,1},{8,10},{9,11},{10,... | collective-permute-start | bytes 786440 | tf_op jit(solution)/shard_map/ppermute | solution.py:39
  89.7 22.8 %collective-permute-start.18 = (bf16[256,1024]{1,0:T(8,128)(2,1)S(1)}, bf16[256,1024]{1,0:T(8,128)(2,1)S(1)}, u32[]{:S(2)}, u32[]{:S(2)}) collective-permute-start(bf16[256,1024]{1,0:T(8,128)(2,1)S(1)} %bitcast.71), channel_id=1, source_target_pairs={{0,2},{1,3},{2,4},{3,5},{4,6},{5,7},{6,0},{7,1},{8,10},{9,11},{10,... | collective-permute-start | bytes 1572872 | tf_op jit(solution)/shard_map/ppermute | solution.py:39
  92.6 19.8 %collective-permute-start.19 = (bf16[256,1024]{1,0:T(8,128)(2,1)S(1)}, bf16[256,1024]{1,0:T(8,128)(2,1)S(1)}, u32[]{:S(2)}, u32[]{:S(2)}) collective-permute-start(bf16[256,1024]{1,0:T(8,128)(2,1)S(1)} %bitcast.72), channel_id=1, source_target_pairs={{0,6},{1,7},{2,0},{3,1},{4,2},{5,3},{6,4},{7,5},{8,14},{9,15},{10,... | collective-permute-start | bytes 1572872 | tf_op jit(solution)/shard_map/ppermute | solution.py:39
  109.5 9.9 %collective-permute-start.14 = (bf16[256,1024]{1,0:T(8,128)(2,1)S(1)}, bf16[256,1024]{1,0:T(8,128)(2,1)S(1)}, u32[]{:S(2)}, u32[]{:S(2)}) collective-permute-start(bf16[256,1024]{1,0:T(8,128)(2,1)S(1)} %get-tuple-element.31), channel_id=1, source_target_pairs={{0,2},{1,3},{2,4},{3,5},{4,6},{5,7},{6,0},{7,1},{8,10},{9,11},{10,... | collective-permute-start | bytes 1572872 | tf_op jit(solution)/shard_map/ppermute | solution.py:39
  109.6 9.8 %collective-permute-start.15 = (bf16[256,1024]{1,0:T(8,128)(2,1)S(1)}, bf16[256,1024]{1,0:T(8,128)(2,1)S(1)}, u32[]{:S(2)}, u32[]{:S(2)}) collective-permute-start(bf16[256,1024]{1,0:T(8,128)(2,1)S(1)} %get-tuple-element.32), channel_id=1, source_target_pairs={{0,6},{1,7},{2,0},{3,1},{4,2},{5,3},{6,4},{7,5},{8,14},{9,15},{10,... | collective-permute-start | bytes 1572872 | tf_op jit(solution)/shard_map/ppermute | solution.py:39
  111.1 6.6 %collective-permute-start.5 = (f32[128,16]{0,1:T(8,128)S(1)}, f32[128,16]{0,1:T(8,128)S(1)}, u32[]{:S(2)}, u32[]{:S(2)}) collective-permute-start(f32[128,16]{0,1:T(8,128)S(1)} %maximum_maximum_fusion.1), channel_id=1, source_target_pairs={{0,2},{1,3},{2,0},{3,1},{4,6},{5,7},{6,4},{7,5},{8,10},{9,11},{10,... | collective-permute-start | bytes 24584 | tf_op jit(solution)/shard_map/ppermute | solution.py:431
  112.5 10.3 %collective-permute-start.20 = (bf16[128,1024]{1,0:T(8,128)(2,1)S(1)}, bf16[128,1024]{1,0:T(8,128)(2,1)S(1)}, u32[]{:S(2)}, u32[]{:S(2)}) collective-permute-start(bf16[128,1024]{1,0:T(8,128)(2,1)S(1)} %get-tuple-element.36), channel_id=1, source_target_pairs={{0,2},{1,3},{2,4},{3,5},{4,6},{5,7},{6,0},{7,1},{8,10},{9,11},{10,... | collective-permute-start | bytes 786440 | tf_op jit(solution)/shard_map/ppermute | solution.py:39
  112.6 10.3 %collective-permute-start.21 = (bf16[128,1024]{1,0:T(8,128)(2,1)S(1)}, bf16[128,1024]{1,0:T(8,128)(2,1)S(1)}, u32[]{:S(2)}, u32[]{:S(2)}) collective-permute-start(bf16[128,1024]{1,0:T(8,128)(2,1)S(1)} %get-tuple-element.37), channel_id=1, source_target_pairs={{0,6},{1,7},{2,0},{3,1},{4,2},{5,3},{6,4},{7,5},{8,14},{9,15},{10,... | collective-permute-start | bytes 786440 | tf_op jit(solution)/shard_map/ppermute | solution.py:39
  117.7 5.1 %collective-permute-start.6 = (f32[128,16]{0,1:T(8,128)S(1)}, f32[128,16]{0,1:T(8,128)S(1)}, u32[]{:S(2)}, u32[]{:S(2)}) collective-permute-start(f32[128,16]{0,1:T(8,128)S(1)} %fusion.103), channel_id=1, source_target_pairs={{0,4},{1,5},{2,6},{3,7},{4,0},{5,1},{6,2},{7,3},{8,12},{9,13},{10,... | collective-permute-start | bytes 24584 | tf_op jit(solution)/shard_map/ppermute | solution.py:432
  119.5 16.3 %collective-permute-start.16 = (bf16[128,1024]{1,0:T(8,128)(2,1)S(1)}, bf16[128,1024]{1,0:T(8,128)(2,1)S(1)}, u32[]{:S(2)}, u32[]{:S(2)}) collective-permute-start(bf16[128,1024]{1,0:T(8,128)(2,1)S(1)} %get-tuple-element.34), channel_id=1, source_target_pairs={{0,2},{1,3},{2,4},{3,5},{4,6},{5,7},{6,0},{7,1},{8,10},{9,11},{10,... | collective-permute-start | bytes 786440 | tf_op jit(solution)/shard_map/ppermute | solution.py:39
  120.6 15.2 %collective-permute-start.17 = (bf16[128,1024]{1,0:T(8,128)(2,1)S(1)}, bf16[128,1024]{1,0:T(8,128)(2,1)S(1)}, u32[]{:S(2)}, u32[]{:S(2)}) collective-permute-start(bf16[128,1024]{1,0:T(8,128)(2,1)S(1)} %get-tuple-element.35), channel_id=1, source_target_pairs={{0,6},{1,7},{2,0},{3,1},{4,2},{5,3},{6,4},{7,5},{8,14},{9,15},{10,... | collective-permute-start | bytes 786440 | tf_op jit(solution)/shard_map/ppermute | solution.py:39
  132.4 0.8 copy-start.5
  133.2 3.6 %copy-start.4 = (bf16[256,1024]{1,0:T(8,128)(2,1)}, bf16[256,1024]{1,0:T(8,128)(2,1)S(1)}, u32[]{:S(2)}) copy-start(bf16[256,1024]{1,0:T(8,128)(2,1)S(1)} %get-tuple-element.40.rest_ref) | copy-start | bytes 1572868
  133.2 10.3 %collective-permute-start.22 = (bf16[256,1024]{1,0:T(8,128)(2,1)S(1)}, bf16[256,1024]{1,0:T(8,128)(2,1)S(1)}, u32[]{:S(2)}, u32[]{:S(2)}) collective-permute-start(bf16[256,1024]{1,0:T(8,128)(2,1)S(1)} %get-tuple-element.41), channel_id=1, source_target_pairs={{0,2},{1,3},{2,4},{3,5},{4,6},{5,7},{6,0},{7,1},{8,10},{9,11},{10,... | collective-permute-start | bytes 1572872 | tf_op jit(solution)/shard_map/ppermute | solution.py:39
  133.6 11.0 %collective-permute-start.23 = (bf16[256,1024]{1,0:T(8,128)(2,1)S(1)}, bf16[256,1024]{1,0:T(8,128)(2,1)S(1)}, u32[]{:S(2)}, u32[]{:S(2)}) collective-permute-start(bf16[256,1024]{1,0:T(8,128)(2,1)S(1)} %get-tuple-element.42), channel_id=1, source_target_pairs={{0,6},{1,7},{2,0},{3,1},{4,2},{5,3},{6,4},{7,5},{8,14},{9,15},{10,... | collective-permute-start | bytes 1572872 | tf_op jit(solution)/shard_map/ppermute | solution.py:39
  136.8 21.9 %all-to-all-start.2 = ((bf16[16,16,1024]{2,1,0:T(8,128)(2,1)}), bf16[16,16,1024]{2,1,0:T(8,128)(2,1)}, u32[]{:S(2)}, u32[]{:S(2)}) async-start(bf16[16,16,1024]{2,1,0:T(8,128)(2,1)} %bitcast.17), calls=%async_computation.2 | async-start | bytes 1048576 | tf_op jit(solution)/shard_map/all_to_all | solution.py:414
  145.7 8.3 %collective-permute-start.24 = (bf16[128,1024]{1,0:T(8,128)(2,1)S(1)}, bf16[128,1024]{1,0:T(8,128)(2,1)S(1)}, u32[]{:S(2)}, u32[]{:S(2)}) collective-permute-start(bf16[128,1024]{1,0:T(8,128)(2,1)S(1)} %get-tuple-element.44), channel_id=1, source_target_pairs={{0,2},{1,3},{2,4},{3,5},{4,6},{5,7},{6,0},{7,1},{8,10},{9,11},{10,... | collective-permute-start | bytes 786440 | tf_op jit(solution)/shard_map/ppermute | solution.py:39
  146.4 9.4 %collective-permute-start.25 = (bf16[128,1024]{1,0:T(8,128)(2,1)S(1)}, bf16[128,1024]{1,0:T(8,128)(2,1)S(1)}, u32[]{:S(2)}, u32[]{:S(2)}) collective-permute-start(bf16[128,1024]{1,0:T(8,128)(2,1)S(1)} %get-tuple-element.45), channel_id=1, source_target_pairs={{0,6},{1,7},{2,0},{3,1},{4,2},{5,3},{6,4},{7,5},{8,14},{9,15},{10,... | collective-permute-start | bytes 786440 | tf_op jit(solution)/shard_map/ppermute | solution.py:39
  154.1 1.8 copy-start.10
  158.7 14.2 %all-to-all-start.4 = ((bf16[16,16,1024]{2,1,0:T(8,128)(2,1)}), bf16[16,16,1024]{2,1,0:T(8,128)(2,1)S(1)}, u32[]{:S(2)}, u32[]{:S(2)}) async-start(bf16[16,16,1024]{2,1,0:T(8,128)(2,1)} %bitcast.22), calls=%async_computation.4 | async-start | bytes 1048576 | tf_op jit(solution)/shard_map/all_to_all | solution.py:414
  172.9 1.0 copy-start.6
  174.0 17.8 %copy-start.9 = (bf16[128,512]{1,0:T(8,128)(2,1)S(1)}, bf16[128,512]{1,0:T(8,128)(2,1)}, u32[]{:S(2)}) copy-start(bf16[128,512]{1,0:T(8,128)(2,1)} %copy-done.8) | copy-start | bytes 393220
  174.0 18.6 %copy-start.1 = (bf16[4096,256]{1,0:T(8,128)(2,1)S(1)}, bf16[4096,256]{1,0:T(8,128)(2,1)}, u32[]{:S(2)}) copy-start(bf16[4096,256]{1,0:T(8,128)(2,1)} %param.20) | copy-start | bytes 6291460
  174.1 17.7 %collective-permute-start.26 = (bf16[128,512]{1,0:T(8,128)(2,1)S(1)}, bf16[128,512]{1,0:T(8,128)(2,1)S(1)}, u32[]{:S(2)}, u32[]{:S(2)}) collective-permute-start(bf16[128,512]{1,0:T(8,128)(2,1)S(1)} %select_convert_fusion), channel_id=1, source_target_pairs={{0,1},{1,0},{2,3},{3,2},{4,5},{5,4},{6,7},{7,6},{8,9},{9,8},{10,11... | collective-permute-start | bytes 393224 | tf_op jit(solution)/shard_map/ppermute | solution.py:43
  (1 other events, 0.7 us)
